TPU v7x, 128 devices: a whole 4x4x4 slice. The times are simulated.
128 devices in a mesh: row: 16 (over y, x_lo, core), col: 8 (over x_hi, z).
Axes of the slice: x: 4 (x_hi: 2, x_lo: 2; x = x_hi * 2 + x_lo), y: 4, z: 4, core: 2. Of those that a mesh axis runs over, the one named last changes fastest.
Arguments:
- tokens: bfloat16 [256, 512, 512], P('row', 'col'), may hold values from -6 to 6
- grad_output: bfloat16 [256, 512, 512], P('row', 'col'), may hold values from -6 to 6
- w_exp: bfloat16 [512, 2048], replicated, may hold values from -0.375 to 0.375
- dw_kernel: float32 [3, 3, 2048], replicated, may hold values from -4.5 to 4.5
- w_proj: bfloat16 [2048, 512], replicated, may hold values from -0.125 to 0.125
- ln_gain: float32 [512], replicated, may hold values from 0.25 to 1.75
- w_qkv: bfloat16 [512, 1536], replicated, may hold values from -16 to 16
- w_out: bfloat16 [512, 512], replicated, may hold values from -0.25 to 0.25
Outputs:
- output: bfloat16 [256, 512, 512], P('row', 'col')
- grad_tokens: bfloat16 [256, 512, 512], P('row', 'col')
All inputs are finite; a program needn't handle non-finite values.
Results may differ from a plain program's by a relative error of at most 0.03.
The roundings to bfloat16 on the way count: a program that leaves them out, or rounds other values in their place, can miss the bound.
Values may be sent and summed in bfloat16 or wider, within the bound.
No kernel may reach another device: no remote copies, remote signals or barrier semaphores. Data moves between devices by JAX's collectives and lax.ppermute only.
A program may use at most 128 MiB of HBM per device.

v0:
```python
import functools

import jax
import jax.numpy as jnp
from jax import lax
from jax.experimental import pallas as pl
from jax.experimental.pallas import tpu as pltpu
from jax.sharding import PartitionSpec as P

C0 = 0.7978845608028654
C1 = C0 * 0.044715
BLK = 256
FRAME = 80
EDGE = 24
LIMIT = 60 * 1024 * 1024


def half_gelu(h):
    h2 = h * h
    return h2, jnp.tanh(h * ((2.0 * C0) + (8.0 * C1) * h2))


def gelu_value(h, t):
    return h + h * t


def double_slope(h, h2, t):
    return (1.0 + t) + (1.0 - t * t) * (h * ((2.0 * C0) + (24.0 * C1) * h2))


def nt(a, b):
    return lax.dot_general(a, b, (((1,), (1,)), ((), ())), preferred_element_type=jnp.float32)


def round_f32(x):
    return x.astype(jnp.bfloat16).astype(jnp.float32)


def lanes_of(part):
    return slice(part * 128, part * 128 + 128)


def put_rows(dst, values, row, count):
    for part in range(BLK // 128):
        dst[part, row : row + count, 8:72, :] = values[:, lanes_of(part)].reshape(count, 64, 128)


def put_edge(dst, values, first, count, col):
    for part in range(BLK // 128):
        for r in range(count):
            dst[part, r, col : col + 1, :] = values[first + r : first + r + 1, lanes_of(part)]


def conv_row(src, part, row, taps):
    total = None
    for a in range(3):
        for b in range(3):
            term = src[part, row + a, 7 + b : 71 + b, :] * taps[a][b]
            total = term if total is None else total + term
    return total


def read_taps(dw, part, flip):
    taps = []
    for a in range(3):
        aa = 2 - a if flip else a
        order = (2, 1, 0) if flip else (0, 1, 2)
        taps.append([0.5 * dw[aa, b : b + 1, lanes_of(part)] for b in order])
    return taps


SLOTS = 8
BLOCK_ROWS = 40
SPAN = 64 * BLOCK_ROWS


def send_order(x, slot, parity):
    k = 8 * slot
    if k:
        x = jnp.concatenate([x[k:], x[:k]], axis=0)
    return pltpu.roll(x, (64 - 4 * parity) & 63, 0)


def receive_order(x, slot, parity):
    k = 8 * slot
    if k:
        x = jnp.concatenate([x[64 - k :], x[: 64 - k]], axis=0)
    return pltpu.roll(x, 4 * parity, 0)


def pack_for_owners(read, parity, packed_rows, out):
    for c in range(4):
        for row in range(16):
            x = send_order(read(row, lanes_of(c)), row % 8, parity)
            packed_rows[c, pl.ds(row // 8 * 512 + row % 8, 64, stride=SLOTS), :] = x
        out[:, lanes_of(c)] = packed_rows[c].astype(jnp.bfloat16)


def grad_att_kernel(place, grad, w_out, out, product, packed_rows):
    product[...] = nt(grad[...], w_out[...])
    pack_for_owners(
        lambda row, lanes: product[row * 64 : row * 64 + 64, lanes], place[0], packed_rows, out
    )


SMEM = pl.BlockSpec(memory_space=pltpu.SMEM)
VMEM = pl.BlockSpec(memory_space=pltpu.VMEM)


def grad_att_for_owners(place, grad, w_out):
    return pl.pallas_call(
        grad_att_kernel,
        out_shape=jax.ShapeDtypeStruct(grad.shape, jnp.bfloat16),
        in_specs=[SMEM, VMEM, VMEM],
        out_specs=VMEM,
        scratch_shapes=[
            pltpu.VMEM(grad.shape, jnp.float32),
            pltpu.VMEM((4, 1024, 128), jnp.float32),
        ],
        name="grad_att",
        compiler_params=pltpu.CompilerParams(vmem_limit_bytes=16 * 1024 * 1024),
    )(place, grad, w_out)


def finish_kernel(place, hidden, attn, out, rows_of):
    for c in range(4):
        rows_of[c] = attn[:, lanes_of(c)].astype(jnp.float32)
        for row in range(16):
            x = rows_of[c, pl.ds(row // 8 * 512 + row % 8, 64, stride=SLOTS), :]
            at = slice(row * 64, row * 64 + 64)
            total = hidden[at, lanes_of(c)].astype(jnp.float32) + receive_order(
                x, row % 8, place[0]
            )
            out[at, lanes_of(c)] = total.astype(jnp.bfloat16)


def finish(place, hidden, attn):
    return pl.pallas_call(
        finish_kernel,
        out_shape=jax.ShapeDtypeStruct(hidden.shape, jnp.bfloat16),
        in_specs=[SMEM, VMEM, VMEM],
        out_specs=VMEM,
        scratch_shapes=[pltpu.VMEM((4, 1024, 128), jnp.float32)],
        name="add_attention",
        compiler_params=pltpu.CompilerParams(vmem_limit_bytes=16 * 1024 * 1024),
    )(place, hidden, attn)


def fwd_kernel(place, top, mid, bot, left, right, w_exp, dw, w_proj, out, sent, act, acc, gout, packed_rows):
    step = pl.program_id(0)
    width = mid.shape[-1]
    w = w_exp[...] * jnp.bfloat16(0.5)

    @pl.when(step == 0)
    def _():
        acc[...] = mid[...].reshape(1024, width).astype(jnp.float32)

    def act_of(x):
        h = jnp.dot(x, w, preferred_element_type=jnp.float32)
        _, t = half_gelu(h)
        return round_f32(gelu_value(h, t))

    put_edge(act, act_of(left[...])[EDGE:], 1, 18, 7)
    put_edge(act, act_of(right[...])[:EDGE], 1, 18, 72)
    put_rows(act, act_of(top[1]), 0, 1)
    for r in range(0, 16, 4):
        put_rows(act, act_of(mid[r : r + 4].reshape(256, width)), 1 + r, 4)
    put_rows(act, act_of(bot[0]), 17, 1)

    for part in range(BLK // 128):
        taps = read_taps(dw, part, False)
        for r in range(16):
            h = conv_row(act, part, r, taps)
            _, t = half_gelu(h)
            gout[r * 64 : r * 64 + 64, lanes_of(part)] = gelu_value(h, t).astype(jnp.bfloat16)
    wp = w_proj[...]
    for r in range(0, 1024, 256):
        acc[r : r + 256] += jnp.dot(gout[r : r + 256], wp, preferred_element_type=jnp.float32)

    @pl.when(step == pl.num_programs(0) - 1)
    def _():
        out[...] = acc[...].astype(jnp.bfloat16)
        pack_for_owners(
            lambda row, lanes: acc[row * 64 : row * 64 + 64, lanes], place[0], packed_rows, sent
        )


def full(shape):
    return pl.BlockSpec(shape, lambda i: (0,) * len(shape))


def forward(place, top, mid, bot, left, right, w_exp, dw, w_proj):
    width, expand = w_exp.shape
    return pl.pallas_call(
        fwd_kernel,
        grid=(expand // BLK,),
        out_shape=(jax.ShapeDtypeStruct((1024, width), jnp.bfloat16),) * 2,
        in_specs=[
            SMEM, full(top.shape), full(mid.shape), full(bot.shape), full(left.shape),
            full(right.shape),
            pl.BlockSpec((width, BLK), lambda i: (0, i)),
            pl.BlockSpec((3, 3, BLK), lambda i: (0, 0, i)),
            pl.BlockSpec((BLK, width), lambda i: (i, 0)),
        ],
        out_specs=(full((1024, width)),) * 2,
        scratch_shapes=[
            pltpu.VMEM((BLK // 128, 18, FRAME, 128), jnp.float32),
            pltpu.VMEM((1024, width), jnp.float32),
            pltpu.VMEM((1024, BLK), jnp.bfloat16),
            pltpu.VMEM((4, 1024, 128), jnp.float32),
        ],
        name="mbconv_forward",
        compiler_params=pltpu.CompilerParams(vmem_limit_bytes=LIMIT),
    )(place, top, mid, bot, left, right, w_exp, dw, w_proj)


def slope_kernel(top, mid, bot, left, near_left, near_right, right, w_exp, dw,
                 pre_out, conv_out, edge_out, act, cols):
    width = mid.shape[-1]
    w = w_exp[...] * jnp.bfloat16(0.5)

    def act_of(x, slope_row=None):
        h = jnp.dot(x, w, preferred_element_type=jnp.float32)
        h2, t = half_gelu(h)
        if slope_row is not None:
            pre_out[slope_row * 64 : slope_row * 64 + x.shape[0], :] = double_slope(h, h2, t)
        return round_f32(gelu_value(h, t))

    for side, pair in enumerate((left, near_left, near_right, right)):
        a = act_of(pair[...])
        for part in range(BLK // 128):
            cols[part, 2 * side : 2 * side + 2, :, :] = a[:, lanes_of(part)].reshape(2, EDGE, 128)
        if side == 0:
            put_edge(act, a[EDGE:], 0, 20, 7)
        if side == 3:
            put_edge(act, a[:EDGE], 0, 20, 72)
    put_rows(act, act_of(top[...].reshape(128, width)), 0, 2)
    for r in range(0, 16, 4):
        put_rows(act, act_of(mid[r : r + 4].reshape(256, width), r), 2 + r, 4)
    put_rows(act, act_of(bot[...].reshape(128, width)), 18, 2)

    for part in range(BLK // 128):
        taps = read_taps(dw, part, False)
        for r in range(18):
            h = conv_row(act, part, r, taps)
            h2, t = half_gelu(h)
            conv_out[r * 64 : r * 64 + 64, lanes_of(part)] = double_slope(h, h2, t)
        for side in range(2):
            h = None
            for a in range(3):
                for b in range(3):
                    term = cols[part, 5 * side + b, a : a + 18, :] * taps[a][b]
                    h = term if h is None else h + term
            h2, t = half_gelu(h)
            edge_out[side * EDGE : side * EDGE + 18, lanes_of(part)] = double_slope(h, h2, t)
            edge_out[side * EDGE + 18 : side * EDGE + EDGE, lanes_of(part)] = jnp.zeros(
                (EDGE - 18, 128), jnp.float32
            )


def slopes(top, mid, bot, left, near_left, near_right, right, w_exp, dw, first, count):
    width = w_exp.shape[0]
    side = full(left.shape)
    rows = (1024, 18 * 64, 2 * EDGE)
    return pl.pallas_call(
        slope_kernel,
        grid=(count,),
        out_shape=tuple(jax.ShapeDtypeStruct((n, count * BLK), jnp.float32) for n in rows),
        in_specs=[
            full(top.shape), full(mid.shape), full(bot.shape), side, side, side, side,
            pl.BlockSpec((width, BLK), lambda i: (0, i + first)),
            pl.BlockSpec((3, 3, BLK), lambda i: (0, 0, i + first)),
        ],
        out_specs=tuple(pl.BlockSpec((n, BLK), lambda i: (0, i)) for n in rows),
        scratch_shapes=[
            pltpu.VMEM((BLK // 128, 20, FRAME, 128), jnp.float32),
            pltpu.VMEM((BLK // 128, 8, EDGE, 128), jnp.float32),
        ],
        name="mbconv_slopes",
        compiler_params=pltpu.CompilerParams(vmem_limit_bytes=LIMIT),
    )(top, mid, bot, left, near_left, near_right, right, w_exp, dw)


def bwd_kernel(split, place, top, grad, back, bot, left, right, *rest):
    tables, rest = rest[:6], rest[6:]
    w_exp, dw, w_proj, out, mixed, pre, acc, rounded, got, ends, sides = rest
    step = pl.program_id(0)

    @pl.when(step == 0)
    def _():
        parity = place[0]
        got[...] = back[...].astype(jnp.float32)

        def tokens_of(half, slot, c):
            return got[pl.ds(half * SPAN + c * 10 + slot, 64, stride=BLOCK_ROWS), :]

        def token_of(half, shift, column, c):
            owner = (column + 128 - shift) & 63
            return got[pl.ds(half * SPAN + owner * BLOCK_ROWS + c * 10 + 9, 1), :]

        for c in range(4):
            lanes = lanes_of(c)
            for row in range(16):
                at = slice(row * 64, row * 64 + 64)
                x = receive_order(tokens_of(row // 8, row % 8, c), row % 8, parity)
                total = grad[at, lanes].astype(jnp.float32) + x
                acc[at, lanes] = total
                rounded[at, lanes] = total.astype(jnp.bfloat16)
            low = receive_order(tokens_of(0, 8, c), 0, 1 - parity)
            ends[64:128, lanes] = (bot[:, lanes].astype(jnp.float32) + low).astype(jnp.bfloat16)
            high = receive_order(tokens_of(1, 8, c), 7, 1 - parity)
            ends[0:64, lanes] = (top[:, lanes].astype(jnp.float32) + high).astype(jnp.bfloat16)
            for side, (halo, column) in enumerate(((left, 63), (right, 0))):
                sides[side, :, lanes] = halo[:, lanes].astype(jnp.float32)
                for i in range(18):
                    half, slot, flip = (i - 1) // 8, (i - 1) % 8, parity
                    if i == 0:
                        half, slot, flip = 1, 7, 1 - parity
                    if i == 17:
                        half, slot, flip = 0, 0, 1 - parity
                    sides[side, i : i + 1, lanes] += token_of(
                        half, 8 * slot + 4 * flip, column, c
                    )

    def work(pre_slope, conv_slope, edge_slope):
        wp = w_proj[...] * jnp.bfloat16(0.5)
        for side, col in enumerate((7, 72)):
            edge = nt(sides[side].astype(jnp.bfloat16), wp)
            edge = edge * edge_slope[side * EDGE : side * EDGE + EDGE]
            put_edge(mixed, round_f32(edge), 0, 18, col)

        def put(x, row, count):
            mid = nt(x, wp) * conv_slope[row * 64 : (row + count) * 64]
            put_rows(mixed, round_f32(mid), row, count)

        put(ends[0:64], 0, 1)
        for r in range(0, 16, 4):
            put(rounded[r * 64 : r * 64 + 256], 1 + r, 4)
        put(ends[64:128], 17, 1)

        for part in range(BLK // 128):
            taps = read_taps(dw, part, True)
            for r in range(16):
                rows = slice(r * 64, r * 64 + 64)
                z = conv_row(mixed, part, r, taps) * pre_slope[rows, lanes_of(part)]
                pre[rows, lanes_of(part)] = z.astype(jnp.bfloat16)
        w = w_exp[...]
        for r in range(0, 1024, 256):
            acc[r : r + 256] += nt(pre[r : r + 256], w)

    @pl.when(step < split)
    def _():
        work(*tables[:3])

    @pl.when(step >= split)
    def _():
        work(*tables[3:])

    @pl.when(step == pl.num_programs(0) - 1)
    def _():
        out[...] = acc[...].astype(jnp.bfloat16)


def backward(place, top, grad, back, bot, left, right, early, late, w_exp, dw, w_proj):
    width, expand = w_exp.shape
    split = early[0].shape[1] // BLK
    return pl.pallas_call(
        functools.partial(bwd_kernel, split),
        grid=(expand // BLK,),
        out_shape=jax.ShapeDtypeStruct((1024, width), jnp.bfloat16),
        in_specs=[
            SMEM, full(top.shape), full(grad.shape), full(back.shape), full(bot.shape),
            full(left.shape), full(right.shape),
            *(pl.BlockSpec((x.shape[0], BLK), lambda i: (0, jnp.minimum(i, split - 1)))
              for x in early),
            *(pl.BlockSpec((x.shape[0], BLK), lambda i: (0, jnp.maximum(i - split, 0)))
              for x in late),
            pl.BlockSpec((width, BLK), lambda i: (0, i)),
            pl.BlockSpec((3, 3, BLK), lambda i: (0, 0, i)),
            pl.BlockSpec((BLK, width), lambda i: (i, 0)),
        ],
        out_specs=full((1024, width)),
        scratch_shapes=[
            pltpu.VMEM((BLK // 128, 18, FRAME, 128), jnp.float32),
            pltpu.VMEM((1024, BLK), jnp.bfloat16),
            pltpu.VMEM((1024, width), jnp.float32),
            pltpu.VMEM((1024, width), jnp.bfloat16),
            pltpu.VMEM(back.shape, jnp.float32),
            pltpu.VMEM((128, width), jnp.bfloat16),
            pltpu.VMEM((2, EDGE, width), jnp.float32),
        ],
        name="mbconv_backward",
        compiler_params=pltpu.CompilerParams(vmem_limit_bytes=LIMIT),
    )(place, top, grad, back, bot, left, right, *early, *late, w_exp, dw, w_proj)


WINDOWS = 16
GROUP = 4
BREADTH = 2


def gather_window(src, start):
    return jnp.concatenate(
        [src[c, pl.ds(start, 64, stride=SLOTS), :] for c in range(4)], axis=1
    )


def scatter_window(dst, start, values):
    for c in range(4):
        dst[c, pl.ds(start, 64, stride=SLOTS), :] = values[:, lanes_of(c)]


def return_slots(place, dst):
    half, owner = place[0], place[1]
    member = lax.broadcasted_iota(jnp.int32, (64, 128), 0)
    for parity in range(2):
        other = 1 - parity
        edge_slot = 7 * half
        row_shift = 1 - half if parity == 1 else -half
        near = owner + 4 * parity
        at_left = (near & 7) == 0
        at_right = (near & 7) == 7
        column = (owner + 8 * edge_slot + 4 * other) & 63
        corner_left = column == 0
        corner_right = column == 63
        side = at_left | at_right
        line = jnp.where(at_left, (64 - near) >> 3, (127 - near) >> 3) & 7
        start = jnp.where(side, parity * SPAN + line, other * SPAN + edge_slot)
        rows_on = jnp.where(side, 0, row_shift)
        cols_on = jnp.where(at_left | corner_left, 1, -1)
        exists = side | corner_left | corner_right
        cases = (
            (8, other * SPAN + edge_slot, row_shift, 0, half >= 0),
            (9, start, rows_on, cols_on, exists),
        )
        for slot, begin, dq, dc, there in cases:
            q = (member >> 3) + dq
            c = (member & 7) + dc
            limit = jnp.where(there, 8, 0)
            valid = (q >= 0) & (q < limit) & (c >= 0) & (c < 8)
            shift = (64 - 8 * dq - dc) & 63
            for chunk in range(4):
                x = dst[pl.ds(begin + chunk * 10, 64, stride=BLOCK_ROWS), :]
                x = jnp.where(valid, pltpu.roll(x, shift, 0), 0.0)
                dst[pl.ds(parity * SPAN + chunk * 10 + slot, 64, stride=BLOCK_ROWS), :] = x


def attend_kernel(place, hid, gatt, gain, w_qkv, back_out, att_out, hs, gs, sends, packed, gpack):
    scale = 32 ** (-0.5)
    for c in range(4):
        hs[c] = hid[:, c * 128 : c * 128 + 128].astype(jnp.float32)
        gs[c] = gatt[:, c * 128 : c * 128 + 128].astype(jnp.float32)
    lane = lax.broadcasted_iota(jnp.int32, (64, 128), 1)
    masks = [(lane >= 32 * h) & (lane < 32 * h + 32) for h in range(4)]
    gain_row = gain[...]

    def spread(x):
        zero = jnp.zeros_like(x)
        return jnp.concatenate([jnp.where(m, x, zero) for m in masks], axis=0)

    def collect(y):
        total = None
        for h in range(4):
            term = jnp.where(masks[h], y[h * 64 : h * 64 + 64], 0.0)
            total = term if total is None else total + term
        return total

    def tn(a, b):
        return lax.dot_general(a, b, (((0,), (0,)), ((), ())), preferred_element_type=jnp.float32)

    def body(group, carry):
        parity, slot = group // 2, (group % 2) * GROUP
        base = parity * 512 + slot
        sent = parity * SPAN + slot
        x = jnp.concatenate([gather_window(hs, base + i) for i in range(GROUP)], axis=0)
        center = x - jnp.mean(x, axis=-1, keepdims=True)
        inv_std = lax.rsqrt(jnp.mean(center * center, axis=-1, keepdims=True) + 1e-5)
        unit = center * inv_std
        normed = (unit * gain_row).astype(jnp.bfloat16)
        packed[...] = jnp.dot(normed, w_qkv[...], preferred_element_type=jnp.float32).astype(
            jnp.bfloat16
        )
        units = [(i, hg) for i in range(GROUP) for hg in range(4)]
        g_all = [gather_window(gs, base + i).astype(jnp.bfloat16) for i in range(GROUP)]
        outs = {}
        for first in range(0, len(units), BREADTH):
            batch = units[first : first + BREADTH]
            st = []
            for i, hg in batch:
                rows = slice(i * 64, i * 64 + 64)
                lo = hg * 128
                k = packed[rows, 512 + lo : 512 + lo + 128]
                v = packed[rows, 1024 + lo : 1024 + lo + 128]
                q_bd = spread(packed[rows, lo : lo + 128])
                g_bd = spread(g_all[i][:, lo : lo + 128])
                st.append((k, v, q_bd, g_bd))
            sd = [(nt(k, q_bd), nt(v, g_bd)) for k, v, q_bd, g_bd in st]
            soft = []
            for s, dp in sd:
                s = s * scale
                e = jnp.exp(s - jnp.max(s, axis=0, keepdims=True))
                p = e * (1.0 / jnp.sum(e, axis=0, keepdims=True))
                dot = jnp.sum(dp * p, axis=0, keepdims=True)
                soft.append((p.astype(jnp.bfloat16), (p * (dp - dot) * scale).astype(jnp.bfloat16)))
            prods = []
            for (k, v, q_bd, g_bd), (p, ds) in zip(st, soft):
                prods.append((
                    jnp.dot(p, g_bd, preferred_element_type=jnp.float32),
                    jnp.dot(ds, q_bd, preferred_element_type=jnp.float32),
                    tn(ds, k),
                    tn(p, v),
                ))
            for (i, hg), (dv, dk, dq, o) in zip(batch, prods):
                rows = slice(i * 64, i * 64 + 64)
                lo = hg * 128
                gpack[rows, lo : lo + 128] = collect(dq).astype(jnp.bfloat16)
                gpack[rows, 512 + lo : 512 + lo + 128] = dk.astype(jnp.bfloat16)
                gpack[rows, 1024 + lo : 1024 + lo + 128] = dv.astype(jnp.bfloat16)
                outs[i, hg] = collect(o)
        for i in range(GROUP):
            scatter_window(gs, base + i, jnp.concatenate([outs[i, hg] for hg in range(4)], axis=1))
        scaled = nt(gpack[...], w_qkv[...]) * gain_row
        grad = inv_std * (
            scaled
            - jnp.mean(scaled, axis=-1, keepdims=True)
            - unit * jnp.mean(scaled * unit, axis=-1, keepdims=True)
        )
        for i in range(GROUP):
            for c in range(4):
                sends[pl.ds(sent + i + c * 10, 64, stride=BLOCK_ROWS), :] = grad[
                    i * 64 : i * 64 + 64, lanes_of(c)
                ]
        return carry

    lax.fori_loop(0, WINDOWS // GROUP, body, 0)
    return_slots(place, sends)
    back_out[...] = sends[...].astype(jnp.bfloat16)
    for c in range(4):
        att_out[:, c * 128 : c * 128 + 128] = gs[c].astype(jnp.bfloat16)


def attend(place, hid, gatt, gain, w_qkv):
    blocks = (128 * BLOCK_ROWS, 128)
    return pl.pallas_call(
        attend_kernel,
        out_shape=(
            jax.ShapeDtypeStruct(blocks, jnp.bfloat16),
            jax.ShapeDtypeStruct(hid.shape, jnp.bfloat16),
        ),
        in_specs=[SMEM] + [VMEM] * 4,
        out_specs=(VMEM, VMEM),
        scratch_shapes=[
            pltpu.VMEM((4, 1024, 128), jnp.float32),
            pltpu.VMEM((4, 1024, 128), jnp.float32),
            pltpu.VMEM(blocks, jnp.float32),
            pltpu.VMEM((GROUP * 64, 1536), jnp.bfloat16),
            pltpu.VMEM((GROUP * 64, 1536), jnp.bfloat16),
        ],
        name="window_attention",
        compiler_params=pltpu.CompilerParams(vmem_limit_bytes=48 * 1024 * 1024),
    )(place, hid, gatt, gain, w_qkv)


def neighbour_pair(axis, size, to_next, to_prev):
    up = [(i, i + 1) for i in range(size - 1)]
    down = [(i + 1, i) for i in range(size - 1)]
    return lax.ppermute(to_next, axis, up), lax.ppermute(to_prev, axis, down)


def edge_columns(parts):
    rows = jnp.concatenate(parts, axis=0).transpose(1, 0, 2)
    rows = jnp.pad(rows, ((0, 0), (0, EDGE - rows.shape[1]), (0, 0)))
    return rows.reshape(-1, rows.shape[2])


EARLY = 5


def per_device(tokens, grad_output, w_exp, dw_kernel, w_proj, ln_gain, w_qkv, w_out):
    rows, cols, width = tokens.shape
    blocks = w_exp.shape[1] // BLK
    row_count = lax.axis_size("row")
    col_count = lax.axis_size("col")
    groups = [
        [
            (2 * q + h) * col_count + c
            for h in range(2)
            for q in range(row_count // 2)
            for c in range(col_count)
        ]
    ]
    row_at, col_at = lax.axis_index("row"), lax.axis_index("col")
    place = jnp.stack([row_at % 2, row_at // 2 * col_count + col_at]).astype(jnp.int32)

    def exchange(flat):
        sent = flat.reshape(row_count * col_count, -1, flat.shape[1])
        moved = lax.all_to_all(
            sent, ("row", "col"), split_axis=0, concat_axis=0, tiled=True,
            axis_index_groups=groups,
        )
        return moved.reshape(flat.shape)

    from_top, from_bot = neighbour_pair(
        "row",
        row_count,
        jnp.concatenate([tokens[rows - 2 :], grad_output[rows - 1 :]], axis=0),
        jnp.concatenate([tokens[:2], grad_output[:1]], axis=0),
    )
    top, g_top, bot, g_bot = from_top[:2], from_top[2:], from_bot[:2], from_bot[2:]
    grad_flat = grad_output.reshape(rows * cols, width)
    grad_win = exchange(grad_att_for_owners(place, grad_flat, w_out))

    near_right = edge_columns([x[:, cols - 2 :] for x in (top, tokens, bot)])
    near_left = edge_columns([x[:, :2] for x in (top, tokens, bot)])
    grad_right = edge_columns([x[:, cols - 1 :] for x in (g_top, grad_output, g_bot)])
    grad_left = edge_columns([x[:, :1] for x in (g_top, grad_output, g_bot)])
    from_left, from_right = neighbour_pair(
        "col",
        col_count,
        jnp.concatenate([near_right, grad_right], axis=0),
        jnp.concatenate([near_left, grad_left], axis=0),
    )
    left, g_left = from_left[: 2 * EDGE], from_left[2 * EDGE :]
    right, g_right = from_right[: 2 * EDGE], from_right[2 * EDGE :]

    hidden, sent = forward(place, top, tokens, bot, left, right, w_exp, dw_kernel, w_proj)
    sent, grad_win = lax.optimization_barrier((sent, grad_win))
    hidden_win = exchange(sent)
    w_late, _ = lax.optimization_barrier((w_exp, sent))
    halo = (top, tokens, bot, left, near_left, near_right, right)
    early = slopes(*halo, w_late, dw_kernel, 0, EARLY)
    hidden_win, *early = lax.optimization_barrier((hidden_win, *early))
    back_win, att_win = attend(place, hidden_win, grad_win, ln_gain.reshape(1, width), w_qkv)
    back = exchange(back_win)
    w_last, att_win = lax.optimization_barrier((w_exp, att_win))
    late = slopes(*halo, w_last, dw_kernel, EARLY, blocks - EARLY)
    attn_win = jnp.dot(att_win, w_out, preferred_element_type=jnp.float32).astype(jnp.bfloat16)
    back, attn_win, *late = lax.optimization_barrier((back, attn_win, *late))
    attn = exchange(attn_win)
    grad_tokens = backward(
        place, g_top.reshape(cols, width), grad_flat, back, g_bot.reshape(cols, width),
        g_left, g_right, early, late, w_exp, dw_kernel, w_proj,
    )
    attn, grad_tokens = lax.optimization_barrier((attn, grad_tokens))
    output = finish(place, hidden, attn)
    return output.reshape(tokens.shape), grad_tokens.reshape(tokens.shape)


def solution(mesh):
    in_specs = (P("row", "col", None), P("row", "col", None), P(), P(), P(), P(), P(), P())
    out_specs = (P("row", "col", None), P("row", "col", None))
    return jax.shard_map(
        per_device, mesh=mesh, in_specs=in_specs, out_specs=out_specs, check_vma=False
    )
```

profile of v0, /device:TPU:7, one launch (start us, length us, event | category | flops | bytes accessed | tf_op | source)
XLA Modules:
  0.0 171.6 jit_solution(6376295571326611030)
XLA Ops:
  0.6 0.0 copy-start
  0.7 1.0 fusion.3
  1.7 0.1 copy.63
  1.8 1.0 fusion.2
  2.8 0.1 copy.62
  2.9 0.3 pad_maximum_fusion
  3.2 4.0 %collective-permute-start = (bf16[3,64,512]{2,0,1:T(4,128)(2,1)S(1)}, bf16[3,64,512]{2,0,1:T(4,128)(2,1)S(1)}, u32[]{:S(2)}, u32[]{:S(2)}) collective-permute-start(bf16[3,64,512]{2,0,1:T(4,128)(2,1)S(1)} %pad_maximum_fusion), channel_id=1, source_target_pairs={{0,8},{8,16},{16,24},{24,32},{32,40},{40,48},{48,56},{56,64},{64,7... | collective-permute-start | bytes 589832 | tf_op jit(solution)/shard_map/ppermute | solution.py:567
  7.2 0.1 copy.65
  7.3 0.1 copy.64
  7.5 1.0 pad_maximum_fusion.1
  8.5 1.9 %collective-permute-start.1 = (bf16[3,64,512]{2,0,1:T(4,128)(2,1)}, bf16[3,64,512]{2,0,1:T(4,128)(2,1)S(1)}, u32[]{:S(2)}, u32[]{:S(2)}) collective-permute-start(bf16[3,64,512]{2,0,1:T(4,128)(2,1)} %pad_maximum_fusion.1), channel_id=1, source_target_pairs={{8,0},{16,8},{24,16},{32,24},{40,32},{48,40},{56,48},{64,56},{72,6... | collective-permute-start | bytes 589832 | tf_op jit(solution)/shard_map/ppermute | solution.py:567
  10.4 0.1 pad_add_fusion.place
  10.5 2.9 %grad_att.1 = bf16[1024,512]{1,0:T(8,128)(2,1)} custom-call(s32[2]{0:T(128)S(1)} %pad_add_fusion.place, bf16[1024,512]{1,0:T(8,128)(2,1)S(1)} %bitcast.37, bf16[512,512]{1,0:T(8,128)(2,1)S(1)} %copy-done.3), custom_call_target="tpu_custom_call" | custom-call | tf_op jit(solution)/shard_map/grad_att/pallas_call | solution.py:111
  13.4 11.3 %all-to-all-start = ((bf16[128,8,512]{2,1,0:T(8,128)(2,1)}), bf16[128,8,512]{2,1,0:T(8,128)(2,1)S(1)}, u32[]{:S(2)}, u32[]{:S(2)}) async-start(bf16[128,8,512]{2,1,0:T(8,128)(2,1)} %bitcast.11), calls=%async_computation | async-start | bytes 2097152 | tf_op jit(solution)/shard_map/all_to_all | solution.py:597
  24.7 0.1 fusion.1
  24.8 1.0 fusion
  26.1 3.3 %collective-permute-start.2 = (bf16[72,512]{1,0:T(8,128)(2,1)S(1)}, bf16[72,512]{1,0:T(8,128)(2,1)S(1)}, u32[]{:S(2)}, u32[]{:S(2)}) collective-permute-start(bf16[72,512]{1,0:T(8,128)(2,1)S(1)} %pad_maximum_fusion.2), channel_id=1, source_target_pairs={{0,1},{1,2},{2,3},{3,4},{4,5},{5,6},{6,7},{8,9},{9,10},{10,11},{11... | collective-permute-start | bytes 221192 | tf_op jit(solution)/shard_map/ppermute | solution.py:567
  29.4 5.6 %collective-permute-start.3 = (bf16[72,512]{1,0:T(8,128)(2,1)S(1)}, bf16[72,512]{1,0:T(8,128)(2,1)S(1)}, u32[]{:S(2)}, u32[]{:S(2)}) collective-permute-start(bf16[72,512]{1,0:T(8,128)(2,1)S(1)} %pad_maximum_fusion.3), channel_id=1, source_target_pairs={{1,0},{2,1},{3,2},{4,3},{5,4},{6,5},{7,6},{9,8},{10,9},{11,10},{12... | collective-permute-start | bytes 221192 | tf_op jit(solution)/shard_map/ppermute | solution.py:567
  35.0 0.1 slice.104
  35.1 0.7 copy.54.top
  35.8 0.1 slice.105
  35.9 0.7 copy.55.bot
  36.6 5.1 %collective-permute-done.2 = bf16[72,512]{1,0:T(8,128)(2,1)S(1)} collective-permute-done((bf16[72,512]{1,0:T(8,128)(2,1)S(1)}, bf16[72,512]{1,0:T(8,128)(2,1)S(1)}, u32[]{:S(2)}, u32[]{:S(2)}) %collective-permute-start.2) | collective-permute-done | bytes 73760 | tf_op jit(solution)/shard_map/ppermute | solution.py:567
  41.7 0.6 slice.110.left
  42.3 0.7 slice.115.right
  43.0 19.9 %mbconv_forward.1 = (bf16[1024,512]{1,0:T(8,128)(2,1)}, bf16[1024,512]{1,0:T(8,128)(2,1)}) custom-call(s32[2]{0:T(128)} %copy-done.4, bf16[2,64,512]{2,1,0:T(8,128)(2,1)} %copy.54.top, bf16[16,64,512]{2,1,0:T(8,128)(2,1)} %mid.5, bf16[2,64,512]{2,1,0:T(8,128)(2,1)} %copy.55.bot, bf16[48,512]{1,0:T(8,128)(2,1)} %slice.110.left, ...), custom_call_target="tpu_custom_call" | custom-call | tf_op jit(solution)/shard_map/mbconv_forward/pallas_call | solution.py:194
  62.9 7.1 %all-to-all-start.1 = ((bf16[128,8,512]{2,1,0:T(8,128)(2,1)}), bf16[128,8,512]{2,1,0:T(8,128)(2,1)S(1)}, u32[]{:S(2)}, u32[]{:S(2)}) async-start(bf16[128,8,512]{2,1,0:T(8,128)(2,1)} %bitcast.44), calls=%async_computation.1 | async-start | bytes 2097152 | tf_op jit(solution)/shard_map/all_to_all | solution.py:597
  70.0 0.0 copy-start.7
  70.0 15.3 %mbconv_slopes.2 = (f32[1024,1280]{1,0:T(8,128)}, f32[1152,1280]{1,0:T(8,128)}, f32[48,1280]{1,0:T(8,128)}) custom-call(bf16[2,64,512]{2,1,0:T(8,128)(2,1)} %copy.54.top, bf16[16,64,512]{2,1,0:T(8,128)(2,1)} %mid.5, bf16[2,64,512]{2,1,0:T(8,128)(2,1)} %copy.55.bot, bf16[48,512]{1,0:T(8,128)(2,1)} %slice.110.left, bf16[48,512]{1,0:T(8,128)(2,1)} %bitcast.50, ...), custom_call_target="tpu_custom_call" | custom-call | tf_op jit(solution)/shard_map/mbconv_slopes/pallas_call | solution.py:265
  85.3 1.8 %all-to-all-done.1 = bf16[128,8,512]{2,1,0:T(8,128)(2,1)S(1)} async-done(((bf16[128,8,512]{2,1,0:T(8,128)(2,1)}), bf16[128,8,512]{2,1,0:T(8,128)(2,1)S(1)}, u32[]{:S(2)}, u32[]{:S(2)}) %all-to-all-start.1) | async-done | bytes 1048608 | tf_op jit(solution)/shard_map/all_to_all | solution.py:597
  87.1 1.4 copy-done.1
  88.5 19.4 %window_attention.1 = (bf16[5120,128]{1,0:T(8,128)(2,1)}, bf16[1024,512]{1,0:T(8,128)(2,1)S(1)}) custom-call(s32[2]{0:T(128)S(1)} %copy-done.5, bf16[1024,512]{1,0:T(8,128)(2,1)S(1)} %bitcast.39, bf16[1024,512]{1,0:T(8,128)(2,1)S(1)} %bitcast.38, f32[1,512]{1,0:T(1,128)S(1)} %bitcast.41, bf16[512,1536]{1,0:T(8,128)(2,1)S(1)} %copy-done.1), custom_call_target="tpu_custom_call" | custom-call | tf_op jit(solution)/shard_map/window_attention/pallas_call | solution.py:544
  108.0 1.0 copy-done.8
  108.9 8.0 %all-to-all-start.2 = ((bf16[128,40,128]{2,1,0:T(8,128)(2,1)}), bf16[128,40,128]{2,1,0:T(8,128)(2,1)S(1)}, u32[]{:S(2)}, u32[]{:S(2)}) async-start(bf16[128,40,128]{2,1,0:T(8,128)(2,1)} %bitcast.16), calls=%async_computation.2 | async-start | bytes 2621440 | tf_op jit(solution)/shard_map/all_to_all | solution.py:597
  117.0 0.0 copy-start.9
  117.0 10.3 %mbconv_slopes.3 = (f32[1024,768]{1,0:T(8,128)}, f32[1152,768]{1,0:T(8,128)}, f32[48,768]{1,0:T(8,128)}) custom-call(bf16[2,64,512]{2,1,0:T(8,128)(2,1)} %copy.54.top, bf16[16,64,512]{2,1,0:T(8,128)(2,1)} %mid.5, bf16[2,64,512]{2,1,0:T(8,128)(2,1)} %copy.55.bot, bf16[48,512]{1,0:T(8,128)(2,1)} %slice.110.left, bf16[48,512]{1,0:T(8,128)(2,1)} %bitcast.51, ...), custom_call_target="tpu_custom_call" | custom-call | tf_op jit(solution)/shard_map/mbconv_slopes/pallas_call | solution.py:265
  127.3 1.7 convolution_convert_fusion
  129.0 7.9 %all-to-all-done.2 = bf16[128,40,128]{2,1,0:T(8,128)(2,1)S(1)} async-done(((bf16[128,40,128]{2,1,0:T(8,128)(2,1)}), bf16[128,40,128]{2,1,0:T(8,128)(2,1)S(1)}, u32[]{:S(2)}, u32[]{:S(2)}) %all-to-all-start.2) | async-done | bytes 1310752 | tf_op jit(solution)/shard_map/all_to_all | solution.py:597
  136.9 1.1 copy-done.10
  137.9 6.5 %all-to-all-start.3 = ((bf16[128,8,512]{2,1,0:T(8,128)(2,1)}), bf16[128,8,512]{2,1,0:T(8,128)(2,1)S(1)}, u32[]{:S(2)}, u32[]{:S(2)}) async-start(bf16[128,8,512]{2,1,0:T(8,128)(2,1)} %bitcast.18), calls=%async_computation.3 | async-start | bytes 2097152 | tf_op jit(solution)/shard_map/all_to_all | solution.py:597
  144.5 0.1 slice.116
  144.6 0.6 copy.73
  145.2 0.1 slice.117
  145.4 0.6 copy.72
  146.0 1.4 slice.118.left
  147.4 1.3 slice.119.right
  148.7 20.6 %mbconv_backward.1 = bf16[1024,512]{1,0:T(8,128)(2,1)} custom-call(s32[2]{0:T(128)} %copy-done.4, bf16[64,512]{1,0:T(8,128)(2,1)} %bitcast.52, bf16[1024,512]{1,0:T(8,128)(2,1)} %bitcast.36, bf16[5120,128]{1,0:T(8,128)(2,1)} %bitcast.42, bf16[64,512]{1,0:T(8,128)(2,1)} %bitcast.53, bf16[24,512]{1,0:T(8,128)(2,1)} %slice.118.left, ...), custom_call_target="tpu_custom_call" | custom-call | tf_op jit(solution)/shard_map/mbconv_backward/pallas_call | solution.py:367
  169.3 2.3 %add_attention.1 = bf16[1024,512]{1,0:T(8,128)(2,1)} custom-call(s32[2]{0:T(128)S(1)} %copy-done.6, bf16[1024,512]{1,0:T(8,128)(2,1)S(1)} %copy-done.2, bf16[1024,512]{1,0:T(8,128)(2,1)S(1)} %bitcast.40), custom_call_target="tpu_custom_call" | custom-call | tf_op jit(solution)/shard_map/add_attention/pallas_call | solution.py:138
  (45 shorter events, 0.2 us)
Async XLA Ops:
  0.6 9.8 %copy-start = (bf16[16,64,512]{2,1,0:T(8,128)(2,1)S(1)}, bf16[16,64,512]{2,1,0:T(8,128)(2,1)}, u32[]{:S(2)}) copy-start(bf16[16,64,512]{2,1,0:T(8,128)(2,1)} %param.9) | copy-start | bytes 3145732
  0.6 9.8 %copy-start.3 = (bf16[512,512]{1,0:T(8,128)(2,1)S(1)}, bf16[512,512]{1,0:T(8,128)(2,1)}, u32[]{:S(2)}) copy-start(bf16[512,512]{1,0:T(8,128)(2,1)} %w_out.1) | copy-start | bytes 1572868
  3.2 22.7 %collective-permute-start = (bf16[3,64,512]{2,0,1:T(4,128)(2,1)S(1)}, bf16[3,64,512]{2,0,1:T(4,128)(2,1)S(1)}, u32[]{:S(2)}, u32[]{:S(2)}) collective-permute-start(bf16[3,64,512]{2,0,1:T(4,128)(2,1)S(1)} %pad_maximum_fusion), channel_id=1, source_target_pairs={{0,8},{8,16},{16,24},{24,32},{32,40},{40,48},{48,56},{56,64},{64,7... | collective-permute-start | bytes 589832 | tf_op jit(solution)/shard_map/ppermute | solution.py:567
  8.5 17.4 %collective-permute-start.1 = (bf16[3,64,512]{2,0,1:T(4,128)(2,1)}, bf16[3,64,512]{2,0,1:T(4,128)(2,1)S(1)}, u32[]{:S(2)}, u32[]{:S(2)}) collective-permute-start(bf16[3,64,512]{2,0,1:T(4,128)(2,1)} %pad_maximum_fusion.1), channel_id=1, source_target_pairs={{8,0},{16,8},{24,16},{32,24},{40,32},{48,40},{56,48},{64,56},{72,6... | collective-permute-start | bytes 589832 | tf_op jit(solution)/shard_map/ppermute | solution.py:567
  10.5 2.9 %copy-start.4 = (s32[2]{0:T(128)}, s32[2]{0:T(128)S(1)}, u32[]{:S(2)}) copy-start(s32[2]{0:T(128)S(1)} %pad_add_fusion.place) | copy-start | bytes 28
  13.4 49.5 %all-to-all-start = ((bf16[128,8,512]{2,1,0:T(8,128)(2,1)}), bf16[128,8,512]{2,1,0:T(8,128)(2,1)S(1)}, u32[]{:S(2)}, u32[]{:S(2)}) async-start(bf16[128,8,512]{2,1,0:T(8,128)(2,1)} %bitcast.11), calls=%async_computation | async-start | bytes 2097152 | tf_op jit(solution)/shard_map/all_to_all | solution.py:597
  26.0 36.9 %copy-start.11 = (bf16[2,24,512]{2,1,0:T(8,128)(2,1)}, bf16[2,24,512]{2,1,0:T(8,128)(2,1)S(1)}, u32[]{:S(2)}) copy-start(bf16[2,24,512]{2,1,0:T(8,128)(2,1)S(1)} %pad.14) | copy-start | bytes 147460
  26.0 36.9 %copy-start.12 = (bf16[2,24,512]{2,1,0:T(8,128)(2,1)}, bf16[2,24,512]{2,1,0:T(8,128)(2,1)S(1)}, u32[]{:S(2)}) copy-start(bf16[2,24,512]{2,1,0:T(8,128)(2,1)S(1)} %pad.16) | copy-start | bytes 147460
  26.1 15.6 %collective-permute-start.2 = (bf16[72,512]{1,0:T(8,128)(2,1)S(1)}, bf16[72,512]{1,0:T(8,128)(2,1)S(1)}, u32[]{:S(2)}, u32[]{:S(2)}) collective-permute-start(bf16[72,512]{1,0:T(8,128)(2,1)S(1)} %pad_maximum_fusion.2), channel_id=1, source_target_pairs={{0,1},{1,2},{2,3},{3,4},{4,5},{5,6},{6,7},{8,9},{9,10},{10,11},{11... | collective-permute-start | bytes 221192 | tf_op jit(solution)/shard_map/ppermute | solution.py:567
  29.4 12.9 %collective-permute-start.3 = (bf16[72,512]{1,0:T(8,128)(2,1)S(1)}, bf16[72,512]{1,0:T(8,128)(2,1)S(1)}, u32[]{:S(2)}, u32[]{:S(2)}) collective-permute-start(bf16[72,512]{1,0:T(8,128)(2,1)S(1)} %pad_maximum_fusion.3), channel_id=1, source_target_pairs={{1,0},{2,1},{3,2},{4,3},{5,4},{6,5},{7,6},{9,8},{10,9},{11,10},{12... | collective-permute-start | bytes 221192 | tf_op jit(solution)/shard_map/ppermute | solution.py:567
  41.7 21.2 %copy-start.13 = (bf16[72,512]{1,0:T(8,128)(2,1)}, bf16[72,512]{1,0:T(8,128)(2,1)S(1)}, u32[]{:S(2)}) copy-start(bf16[72,512]{1,0:T(8,128)(2,1)S(1)} %collective-permute-done.2) | copy-start | bytes 221188
  42.3 20.5 %copy-start.14 = (bf16[72,512]{1,0:T(8,128)(2,1)}, bf16[72,512]{1,0:T(8,128)(2,1)S(1)}, u32[]{:S(2)}) copy-start(bf16[72,512]{1,0:T(8,128)(2,1)S(1)} %collective-permute-done.3) | copy-start | bytes 221188
  62.9 24.2 %all-to-all-start.1 = ((bf16[128,8,512]{2,1,0:T(8,128)(2,1)}), bf16[128,8,512]{2,1,0:T(8,128)(2,1)S(1)}, u32[]{:S(2)}, u32[]{:S(2)}) async-start(bf16[128,8,512]{2,1,0:T(8,128)(2,1)} %bitcast.44), calls=%async_computation.1 | async-start | bytes 2097152 | tf_op jit(solution)/shard_map/all_to_all | solution.py:597
  70.0 17.1 %copy-start.5 = (s32[2]{0:T(128)S(1)}, s32[2]{0:T(128)}, u32[]{:S(2)}) copy-start(s32[2]{0:T(128)} %copy-done.4) | copy-start | bytes 28
  70.0 17.1 %copy-start.7 = (f32[512]{0:T(512)S(1)}, f32[512]{0:T(512)}, u32[]{:S(2)}) copy-start(f32[512]{0:T(512)} %param.13) | copy-start | bytes 6148
  87.1 1.4 copy-start.1
  108.0 1.0 copy-start.8
  108.9 27.9 %all-to-all-start.2 = ((bf16[128,40,128]{2,1,0:T(8,128)(2,1)}), bf16[128,40,128]{2,1,0:T(8,128)(2,1)S(1)}, u32[]{:S(2)}, u32[]{:S(2)}) async-start(bf16[128,40,128]{2,1,0:T(8,128)(2,1)} %bitcast.16), calls=%async_computation.2 | async-start | bytes 2621440 | tf_op jit(solution)/shard_map/all_to_all | solution.py:597
  117.0 10.3 %copy-start.9 = (bf16[1024,512]{1,0:T(8,128)(2,1)S(1)}, bf16[1024,512]{1,0:T(8,128)(2,1)}, u32[]{:S(2)}) copy-start(bf16[1024,512]{1,0:T(8,128)(2,1)} %copy-done.8) | copy-start | bytes 3145732
  136.8 1.1 copy-start.10
  137.9 31.4 %all-to-all-start.3 = ((bf16[128,8,512]{2,1,0:T(8,128)(2,1)}), bf16[128,8,512]{2,1,0:T(8,128)(2,1)S(1)}, u32[]{:S(2)}, u32[]{:S(2)}) async-start(bf16[128,8,512]{2,1,0:T(8,128)(2,1)} %bitcast.18), calls=%async_computation.3 | async-start | bytes 2097152 | tf_op jit(solution)/shard_map/all_to_all | solution.py:597
  148.7 20.6 %copy-start.2 = (bf16[1024,512]{1,0:T(8,128)(2,1)S(1)}, bf16[1024,512]{1,0:T(8,128)(2,1)}, u32[]{:S(2)}) copy-start(bf16[1024,512]{1,0:T(8,128)(2,1)} %get-tuple-element.28.hidden) | copy-start | bytes 3145732
  148.7 20.6 %copy-start.6 = (s32[2]{0:T(128)S(1)}, s32[2]{0:T(128)}, u32[]{:S(2)}) copy-start(s32[2]{0:T(128)} %copy-done.4) | copy-start | bytes 28
where the time goes:
time: 173 us; the launch traced here: 172 us
  Pallas kernels  90.7 us (52%)
  starting transfers between devices  47.8 us (28%)
  waiting for transfers between devices  14.8 us (9%)
  local copies, waits for them, and re-layouts  14.2 us (8%)
    all_to_all x4, starting transfers between devices, exchange(): lax.all_to_all(sent, ('row', 'col'), split_axis=0, concat_axis=0, tiled=T...  32.9 us
    pallas_call x2, Pallas kernels, slopes(): pl.pallas_call(slope_kernel, grid=(count,), out_shape=tuple((jax.ShapeDty...  25.6 us
    pallas_call x1, Pallas kernels, backward(): pl.pallas_call(functools.partial(bwd_kernel, split), grid=(expand // BLK,...  20.6 us
    pallas_call x1, Pallas kernels, forward(): pl.pallas_call(fwd_kernel, grid=(expand // BLK,), out_shape=(jax.ShapeDty...  19.9 us
    pallas_call x1, Pallas kernels, attend(): pl.pallas_call(attend_kernel, out_shape=(jax.ShapeDtypeStruct(blocks, jnp...  19.4 us
    ppermute x4, starting transfers between devices, neighbour_pair(): return (lax.ppermute(to_next, axis, up), lax.ppermute(to_prev, axis, down))  14.8 us
    all_to_all x4, waiting for transfers between devices, exchange(): lax.all_to_all(sent, ('row', 'col'), split_axis=0, concat_axis=0, tiled=T...  9.66 us
    unnamed x40, local copies, waits for them, and re-layouts  5.28 us
  transfers between devices with their start and end apart: 8, of which 3 were waited for; matrix products, arithmetic and copies ran while one was open for 7% of the time, Pallas kernels for 40%

commit v1 on v0

--- a/solution.py
+++ b/solution.py
@@ -1,11 +1,10 @@
-import functools
-
 import jax
 import jax.numpy as jnp
 from jax import lax
 from jax.experimental import pallas as pl
 from jax.experimental.pallas import tpu as pltpu
 from jax.sharding import PartitionSpec as P
+
 
 C0 = 0.7978845608028654
 C1 = C0 * 0.044715
@@ -160,8 +159,8 @@
         _, t = half_gelu(h)
         return round_f32(gelu_value(h, t))
 
-    put_edge(act, act_of(left[...])[EDGE:], 1, 18, 7)
-    put_edge(act, act_of(right[...])[:EDGE], 1, 18, 72)
+    put_edge(act, act_of(left[: 2 * EDGE])[EDGE:], 1, 18, 7)
+    put_edge(act, act_of(right[: 2 * EDGE])[:EDGE], 1, 18, 72)
     put_rows(act, act_of(top[1]), 0, 1)
     for r in range(0, 16, 4):
         put_rows(act, act_of(mid[r : r + 4].reshape(256, width)), 1 + r, 4)
@@ -214,8 +213,8 @@
     )(place, top, mid, bot, left, right, w_exp, dw, w_proj)
 
 
-def slope_kernel(top, mid, bot, left, near_left, near_right, right, w_exp, dw,
-                 pre_out, conv_out, edge_out, act, cols):
+def slope_kernel(top, mid, bot, left, near_left, near_right, right, w_exp, dw, *rest):
+    pre_out, conv_out, edge_out, act, cols = rest[-5:]
     width = mid.shape[-1]
     w = w_exp[...] * jnp.bfloat16(0.5)
 
@@ -227,17 +226,17 @@
         return round_f32(gelu_value(h, t))
 
     for side, pair in enumerate((left, near_left, near_right, right)):
-        a = act_of(pair[...])
+        a = act_of(pair[: 2 * EDGE])
         for part in range(BLK // 128):
             cols[part, 2 * side : 2 * side + 2, :, :] = a[:, lanes_of(part)].reshape(2, EDGE, 128)
         if side == 0:
             put_edge(act, a[EDGE:], 0, 20, 7)
         if side == 3:
             put_edge(act, a[:EDGE], 0, 20, 72)
-    put_rows(act, act_of(top[...].reshape(128, width)), 0, 2)
+    put_rows(act, act_of(top[:2].reshape(128, width)), 0, 2)
     for r in range(0, 16, 4):
         put_rows(act, act_of(mid[r : r + 4].reshape(256, width), r), 2 + r, 4)
-    put_rows(act, act_of(bot[...].reshape(128, width)), 18, 2)
+    put_rows(act, act_of(bot[:2].reshape(128, width)), 18, 2)
 
     for part in range(BLK // 128):
         taps = read_taps(dw, part, False)
@@ -258,32 +257,33 @@
             )
 
 
-def slopes(top, mid, bot, left, near_left, near_right, right, w_exp, dw, first, count):
-    width = w_exp.shape[0]
-    side = full(left.shape)
+def slopes(top, mid, bot, left, near_left, near_right, right, w_exp, dw, first, count, done=()):
+    width, expand = w_exp.shape
     rows = (1024, 18 * 64, 2 * EDGE)
+    operands = (top, mid, bot, left, near_left, near_right, right)
     return pl.pallas_call(
         slope_kernel,
         grid=(count,),
-        out_shape=tuple(jax.ShapeDtypeStruct((n, count * BLK), jnp.float32) for n in rows),
+        out_shape=tuple(jax.ShapeDtypeStruct((n, expand), jnp.float32) for n in rows),
         in_specs=[
-            full(top.shape), full(mid.shape), full(bot.shape), side, side, side, side,
+            *(full(x.shape) for x in operands),
             pl.BlockSpec((width, BLK), lambda i: (0, i + first)),
             pl.BlockSpec((3, 3, BLK), lambda i: (0, 0, i + first)),
-        ],
-        out_specs=tuple(pl.BlockSpec((n, BLK), lambda i: (0, i)) for n in rows),
+            *(pl.BlockSpec(memory_space=pl.ANY) for _ in done),
+        ],
+        out_specs=tuple(pl.BlockSpec((n, BLK), lambda i: (0, i + first)) for n in rows),
+        input_output_aliases={9 + i: i for i in range(len(done))},
         scratch_shapes=[
             pltpu.VMEM((BLK // 128, 20, FRAME, 128), jnp.float32),
             pltpu.VMEM((BLK // 128, 8, EDGE, 128), jnp.float32),
         ],
         name="mbconv_slopes",
         compiler_params=pltpu.CompilerParams(vmem_limit_bytes=LIMIT),
-    )(top, mid, bot, left, near_left, near_right, right, w_exp, dw)
-
-
-def bwd_kernel(split, place, top, grad, back, bot, left, right, *rest):
-    tables, rest = rest[:6], rest[6:]
-    w_exp, dw, w_proj, out, mixed, pre, acc, rounded, got, ends, sides = rest
+    )(*operands, w_exp, dw, *done)
+
+
+def bwd_kernel(place, top, grad, back, bot, left, right, pre_slope, conv_slope, edge_slope,
+               w_exp, dw, w_proj, out, mixed, pre, acc, rounded, got, ends, sides):
     step = pl.program_id(0)
 
     @pl.when(step == 0)
@@ -307,11 +307,11 @@
                 acc[at, lanes] = total
                 rounded[at, lanes] = total.astype(jnp.bfloat16)
             low = receive_order(tokens_of(0, 8, c), 0, 1 - parity)
-            ends[64:128, lanes] = (bot[:, lanes].astype(jnp.float32) + low).astype(jnp.bfloat16)
+            ends[64:128, lanes] = (bot[2, :, lanes].astype(jnp.float32) + low).astype(jnp.bfloat16)
             high = receive_order(tokens_of(1, 8, c), 7, 1 - parity)
-            ends[0:64, lanes] = (top[:, lanes].astype(jnp.float32) + high).astype(jnp.bfloat16)
+            ends[0:64, lanes] = (top[2, :, lanes].astype(jnp.float32) + high).astype(jnp.bfloat16)
             for side, (halo, column) in enumerate(((left, 63), (right, 0))):
-                sides[side, :, lanes] = halo[:, lanes].astype(jnp.float32)
+                sides[side, :, lanes] = halo[:, lanes].astype(jnp.float32)[2 * EDGE :]
                 for i in range(18):
                     half, slot, flip = (i - 1) // 8, (i - 1) % 8, parity
                     if i == 0:
@@ -322,59 +322,46 @@
                         half, 8 * slot + 4 * flip, column, c
                     )
 
-    def work(pre_slope, conv_slope, edge_slope):
-        wp = w_proj[...] * jnp.bfloat16(0.5)
-        for side, col in enumerate((7, 72)):
-            edge = nt(sides[side].astype(jnp.bfloat16), wp)
-            edge = edge * edge_slope[side * EDGE : side * EDGE + EDGE]
-            put_edge(mixed, round_f32(edge), 0, 18, col)
-
-        def put(x, row, count):
-            mid = nt(x, wp) * conv_slope[row * 64 : (row + count) * 64]
-            put_rows(mixed, round_f32(mid), row, count)
-
-        put(ends[0:64], 0, 1)
-        for r in range(0, 16, 4):
-            put(rounded[r * 64 : r * 64 + 256], 1 + r, 4)
-        put(ends[64:128], 17, 1)
-
-        for part in range(BLK // 128):
-            taps = read_taps(dw, part, True)
-            for r in range(16):
-                rows = slice(r * 64, r * 64 + 64)
-                z = conv_row(mixed, part, r, taps) * pre_slope[rows, lanes_of(part)]
-                pre[rows, lanes_of(part)] = z.astype(jnp.bfloat16)
-        w = w_exp[...]
-        for r in range(0, 1024, 256):
-            acc[r : r + 256] += nt(pre[r : r + 256], w)
-
-    @pl.when(step < split)
-    def _():
-        work(*tables[:3])
-
-    @pl.when(step >= split)
-    def _():
-        work(*tables[3:])
+    wp = w_proj[...] * jnp.bfloat16(0.5)
+    for side, col in enumerate((7, 72)):
+        edge = nt(sides[side].astype(jnp.bfloat16), wp)
+        edge = edge * edge_slope[side * EDGE : side * EDGE + EDGE]
+        put_edge(mixed, round_f32(edge), 0, 18, col)
+
+    def put(x, row, count):
+        mid = nt(x, wp) * conv_slope[row * 64 : (row + count) * 64]
+        put_rows(mixed, round_f32(mid), row, count)
+
+    put(ends[0:64], 0, 1)
+    for r in range(0, 16, 4):
+        put(rounded[r * 64 : r * 64 + 256], 1 + r, 4)
+    put(ends[64:128], 17, 1)
+
+    for part in range(BLK // 128):
+        taps = read_taps(dw, part, True)
+        for r in range(16):
+            rows = slice(r * 64, r * 64 + 64)
+            z = conv_row(mixed, part, r, taps) * pre_slope[rows, lanes_of(part)]
+            pre[rows, lanes_of(part)] = z.astype(jnp.bfloat16)
+    w = w_exp[...]
+    for r in range(0, 1024, 256):
+        acc[r : r + 256] += nt(pre[r : r + 256], w)
 
     @pl.when(step == pl.num_programs(0) - 1)
     def _():
         out[...] = acc[...].astype(jnp.bfloat16)
 
 
-def backward(place, top, grad, back, bot, left, right, early, late, w_exp, dw, w_proj):
+def backward(place, top, grad, back, bot, left, right, tables, w_exp, dw, w_proj):
     width, expand = w_exp.shape
-    split = early[0].shape[1] // BLK
     return pl.pallas_call(
-        functools.partial(bwd_kernel, split),
+        bwd_kernel,
         grid=(expand // BLK,),
         out_shape=jax.ShapeDtypeStruct((1024, width), jnp.bfloat16),
         in_specs=[
             SMEM, full(top.shape), full(grad.shape), full(back.shape), full(bot.shape),
             full(left.shape), full(right.shape),
-            *(pl.BlockSpec((x.shape[0], BLK), lambda i: (0, jnp.minimum(i, split - 1)))
-              for x in early),
-            *(pl.BlockSpec((x.shape[0], BLK), lambda i: (0, jnp.maximum(i - split, 0)))
-              for x in late),
+            *(pl.BlockSpec((x.shape[0], BLK), lambda i: (0, i)) for x in tables),
             pl.BlockSpec((width, BLK), lambda i: (0, i)),
             pl.BlockSpec((3, 3, BLK), lambda i: (0, 0, i)),
             pl.BlockSpec((BLK, width), lambda i: (i, 0)),
@@ -391,7 +378,7 @@
         ],
         name="mbconv_backward",
         compiler_params=pltpu.CompilerParams(vmem_limit_bytes=LIMIT),
-    )(place, top, grad, back, bot, left, right, *early, *late, w_exp, dw, w_proj)
+    )(place, top, grad, back, bot, left, right, *tables, w_exp, dw, w_proj)
 
 
 WINDOWS = 16
@@ -576,7 +563,7 @@
 EARLY = 5
 
 
-def per_device(tokens, grad_output, w_exp, dw_kernel, w_proj, ln_gain, w_qkv, w_out):
+def device_work(tokens, grad_output, w_exp, dw_kernel, w_proj, ln_gain, w_qkv, w_out):
     rows, cols, width = tokens.shape
     blocks = w_exp.shape[1] // BLK
     row_count = lax.axis_size("row")
@@ -608,38 +595,37 @@
     )
     top, g_top, bot, g_bot = from_top[:2], from_top[2:], from_bot[:2], from_bot[2:]
     grad_flat = grad_output.reshape(rows * cols, width)
-    grad_win = exchange(grad_att_for_owners(place, grad_flat, w_out))
+    grad_att = grad_att_for_owners(place, grad_flat, w_out)
 
     near_right = edge_columns([x[:, cols - 2 :] for x in (top, tokens, bot)])
     near_left = edge_columns([x[:, :2] for x in (top, tokens, bot)])
     grad_right = edge_columns([x[:, cols - 1 :] for x in (g_top, grad_output, g_bot)])
     grad_left = edge_columns([x[:, :1] for x in (g_top, grad_output, g_bot)])
-    from_left, from_right = neighbour_pair(
-        "col",
-        col_count,
-        jnp.concatenate([near_right, grad_right], axis=0),
-        jnp.concatenate([near_left, grad_left], axis=0),
+    to_right = jnp.concatenate([near_right, grad_right], axis=0)
+    to_left = jnp.concatenate([near_left, grad_left], axis=0)
+    to_right, to_left, grad_att = lax.optimization_barrier((to_right, to_left, grad_att))
+    from_left, from_right = neighbour_pair("col", col_count, to_right, to_left)
+    grad_win = exchange(grad_att)
+
+    hidden, sent = forward(
+        place, from_top, tokens, from_bot, from_left, from_right, w_exp, dw_kernel, w_proj
     )
-    left, g_left = from_left[: 2 * EDGE], from_left[2 * EDGE :]
-    right, g_right = from_right[: 2 * EDGE], from_right[2 * EDGE :]
-
-    hidden, sent = forward(place, top, tokens, bot, left, right, w_exp, dw_kernel, w_proj)
     sent, grad_win = lax.optimization_barrier((sent, grad_win))
     hidden_win = exchange(sent)
     w_late, _ = lax.optimization_barrier((w_exp, sent))
-    halo = (top, tokens, bot, left, near_left, near_right, right)
-    early = slopes(*halo, w_late, dw_kernel, 0, EARLY)
-    hidden_win, *early = lax.optimization_barrier((hidden_win, *early))
+    halo = (from_top, tokens, from_bot, from_left, near_left, near_right, from_right)
+    tables = slopes(*halo, w_late, dw_kernel, 0, EARLY)
+    hidden_win, *tables = lax.optimization_barrier((hidden_win, *tables))
     back_win, att_win = attend(place, hidden_win, grad_win, ln_gain.reshape(1, width), w_qkv)
     back = exchange(back_win)
     w_last, att_win = lax.optimization_barrier((w_exp, att_win))
-    late = slopes(*halo, w_last, dw_kernel, EARLY, blocks - EARLY)
+    tables = slopes(*halo, w_last, dw_kernel, EARLY, blocks - EARLY, tables)
     attn_win = jnp.dot(att_win, w_out, preferred_element_type=jnp.float32).astype(jnp.bfloat16)
-    back, attn_win, *late = lax.optimization_barrier((back, attn_win, *late))
+    back, attn_win, *tables = lax.optimization_barrier((back, attn_win, *tables))
     attn = exchange(attn_win)
     grad_tokens = backward(
-        place, g_top.reshape(cols, width), grad_flat, back, g_bot.reshape(cols, width),
-        g_left, g_right, early, late, w_exp, dw_kernel, w_proj,
+        place, from_top, grad_flat, back, from_bot, from_left, from_right, tables,
+        w_exp, dw_kernel, w_proj,
     )
     attn, grad_tokens = lax.optimization_barrier((attn, grad_tokens))
     output = finish(place, hidden, attn)
@@ -650,5 +636,5 @@
     in_specs = (P("row", "col", None), P("row", "col", None), P(), P(), P(), P(), P(), P())
     out_specs = (P("row", "col", None), P("row", "col", None))
     return jax.shard_map(
-        per_device, mesh=mesh, in_specs=in_specs, out_specs=out_specs, check_vma=False
+        device_work, mesh=mesh, in_specs=in_specs, out_specs=out_specs, check_vma=False
     )

time: 173 us -> 169 us (0.977)
  local copies, waits for them, and re-layouts: 14.2 us -> 9.84 us
  waiting for transfers between devices: 14.8 us -> 18.6 us
    slice x18 -> x8, local copies, waits for them, and re-layouts: 8.92 us -> 3.1 us  [the longest x3 1.04 us: device_work(): near_left = edge_columns([x[:, :2] for x in (top, tokens, bot)])]
    ppermute x4, waiting for transfers between devices: 5.1 us -> 9.07 us  [neighbour_pair(): return (lax.ppermute(to_next, axis, up), lax.ppermute(to_prev, axis, down))]
    unnamed x40 -> x38, local copies, waits for them, and re-layouts: 5.28 us -> 5.24 us
  transfers between devices with their start and end apart: 8 -> 8, of which waited for: 3 -> 4; matrix products, arithmetic and copies ran while one was open for 7% -> 3% of each run, Pallas kernels for 40% -> 41%
where the time goes in v1:
time: 169 us; the launch traced here: 168 us
  Pallas kernels  90 us (53%)
  starting transfers between devices  46.1 us (27%)
  waiting for transfers between devices  18.6 us (11%)
  local copies, waits for them, and re-layouts  9.84 us (6%)
  matrix products  1.7 us (1%)
    all_to_all x4, starting transfers between devices, exchange(): lax.all_to_all(sent, ('row', 'col'), split_axis=0, concat_axis=0, tiled=T...  31.2 us
    pallas_call x2, Pallas kernels, slopes(): pl.pallas_call(slope_kernel, grid=(count,), out_shape=tuple((jax.ShapeDty...  25.7 us
    pallas_call x1, Pallas kernels, forward(): pl.pallas_call(fwd_kernel, grid=(expand // BLK,), out_shape=(jax.ShapeDty...  19.9 us
    pallas_call x1, Pallas kernels, backward(): pl.pallas_call(bwd_kernel, grid=(expand // BLK,), out_shape=jax.ShapeDtyp...  19.7 us
    pallas_call x1, Pallas kernels, attend(): pl.pallas_call(attend_kernel, out_shape=(jax.ShapeDtypeStruct(blocks, jnp...  19.5 us
    ppermute x4, starting transfers between devices, neighbour_pair(): return (lax.ppermute(to_next, axis, up), lax.ppermute(to_prev, axis, down))  14.8 us
    all_to_all x4, waiting for transfers between devices, exchange(): lax.all_to_all(sent, ('row', 'col'), split_axis=0, concat_axis=0, tiled=T...  9.58 us
    ppermute x4, waiting for transfers between devices, neighbour_pair(): return (lax.ppermute(to_next, axis, up), lax.ppermute(to_prev, axis, down))  9.07 us
  transfers between devices with their start and end apart: 8, of which 4 were waited for; matrix products, arithmetic and copies ran while one was open for 3% of the time, Pallas kernels for 41%

profile of v1, /device:TPU:7, one launch (start us, length us, event | category | flops | bytes accessed | tf_op | source)
XLA Modules:
  0.0 168.0 jit_solution(11046874150697107905)
XLA Ops:
  0.6 0.0 copy-start
  0.7 1.0 fusion.3
  1.7 0.1 copy.50
  1.8 1.0 fusion.2
  2.8 0.1 copy.49
  2.9 0.3 pad_maximum_fusion
  3.2 4.0 %collective-permute-start = (bf16[3,64,512]{2,0,1:T(4,128)(2,1)S(1)}, bf16[3,64,512]{2,0,1:T(4,128)(2,1)S(1)}, u32[]{:S(2)}, u32[]{:S(2)}) collective-permute-start(bf16[3,64,512]{2,0,1:T(4,128)(2,1)S(1)} %pad_maximum_fusion), channel_id=1, source_target_pairs={{0,8},{8,16},{16,24},{24,32},{32,40},{40,48},{48,56},{56,64},{64,7... | collective-permute-start | bytes 589832 | tf_op jit(solution)/shard_map/ppermute | solution.py:554
  7.2 0.1 copy.52
  7.3 0.1 copy.51
  7.5 0.3 pad_maximum_fusion.1
  7.8 1.9 %collective-permute-start.1 = (bf16[3,64,512]{2,0,1:T(4,128)(2,1)S(1)}, bf16[3,64,512]{2,0,1:T(4,128)(2,1)S(1)}, u32[]{:S(2)}, u32[]{:S(2)}) collective-permute-start(bf16[3,64,512]{2,0,1:T(4,128)(2,1)S(1)} %pad_maximum_fusion.1), channel_id=1, source_target_pairs={{8,0},{16,8},{24,16},{32,24},{40,32},{48,40},{56,48},{64,56},{72,6... | collective-permute-start | bytes 589832 | tf_op jit(solution)/shard_map/ppermute | solution.py:554
  9.7 0.1 fusion.1
  9.8 1.0 fusion
  10.9 0.1 pad_add_fusion.place
  11.0 0.0 copy-done.3
  11.0 2.9 %grad_att.1 = bf16[1024,512]{1,0:T(8,128)(2,1)} custom-call(s32[2]{0:T(128)S(1)} %pad_add_fusion.place, bf16[1024,512]{1,0:T(8,128)(2,1)S(1)} %bitcast.31, bf16[512,512]{1,0:T(8,128)(2,1)S(1)} %copy-done.3), custom_call_target="tpu_custom_call" | custom-call | tf_op jit(solution)/shard_map/grad_att/pallas_call | solution.py:110
  13.9 2.5 %collective-permute-done.1 = bf16[3,64,512]{2,0,1:T(4,128)(2,1)S(1)} collective-permute-done((bf16[3,64,512]{2,0,1:T(4,128)(2,1)S(1)}, bf16[3,64,512]{2,0,1:T(4,128)(2,1)S(1)}, u32[]{:S(2)}, u32[]{:S(2)}) %collective-permute-start.1) | collective-permute-done | bytes 196640 | tf_op jit(solution)/shard_map/ppermute | solution.py:554
  16.4 0.0 collective-permute-done
  16.6 9.6 %all-to-all-start = ((bf16[128,8,512]{2,1,0:T(8,128)(2,1)}), bf16[128,8,512]{2,1,0:T(8,128)(2,1)S(1)}, u32[]{:S(2)}, u32[]{:S(2)}) async-start(bf16[128,8,512]{2,1,0:T(8,128)(2,1)} %bitcast.11), calls=%async_computation | async-start | bytes 2097152 | tf_op jit(solution)/shard_map/all_to_all | solution.py:584
  26.3 3.3 %collective-permute-start.2 = (bf16[72,512]{1,0:T(8,128)(2,1)S(1)}, bf16[72,512]{1,0:T(8,128)(2,1)S(1)}, u32[]{:S(2)}, u32[]{:S(2)}) collective-permute-start(bf16[72,512]{1,0:T(8,128)(2,1)S(1)} %pad_maximum_fusion.2), channel_id=1, source_target_pairs={{0,1},{1,2},{2,3},{3,4},{4,5},{5,6},{6,7},{8,9},{9,10},{10,11},{11... | collective-permute-start | bytes 221192 | tf_op jit(solution)/shard_map/ppermute | solution.py:554
  29.5 5.6 %collective-permute-start.3 = (bf16[72,512]{1,0:T(8,128)(2,1)S(1)}, bf16[72,512]{1,0:T(8,128)(2,1)S(1)}, u32[]{:S(2)}, u32[]{:S(2)}) collective-permute-start(bf16[72,512]{1,0:T(8,128)(2,1)S(1)} %pad_maximum_fusion.3), channel_id=1, source_target_pairs={{1,0},{2,1},{3,2},{4,3},{5,4},{6,5},{7,6},{9,8},{10,9},{11,10},{12... | collective-permute-start | bytes 221192 | tf_op jit(solution)/shard_map/ppermute | solution.py:554
  35.2 0.7 copy.41.top
  35.9 0.8 copy.42.bot
  36.6 6.6 %collective-permute-done.2.left = bf16[72,512]{1,0:T(8,128)(2,1)S(1)} collective-permute-done((bf16[72,512]{1,0:T(8,128)(2,1)S(1)}, bf16[72,512]{1,0:T(8,128)(2,1)S(1)}, u32[]{:S(2)}, u32[]{:S(2)}) %collective-permute-start.2) | collective-permute-done | bytes 73760 | tf_op jit(solution)/shard_map/ppermute | solution.py:554
  43.3 0.0 collective-permute-done.3.right
  43.3 0.6 copy-done.11
  43.9 0.6 copy-done.12
  44.5 19.9 %mbconv_forward.1 = (bf16[1024,512]{1,0:T(8,128)(2,1)}, bf16[1024,512]{1,0:T(8,128)(2,1)}) custom-call(s32[2]{0:T(128)} %copy-done.4, bf16[3,64,512]{2,1,0:T(8,128)(2,1)} %copy.41.top, bf16[16,64,512]{2,1,0:T(8,128)(2,1)} %mid.5, bf16[3,64,512]{2,1,0:T(8,128)(2,1)} %copy.42.bot, bf16[72,512]{1,0:T(8,128)(2,1)} %copy-done.11, bf16[72,512]{1,0:T(8,128)(2,1)} %copy-done.12, ...), custom_call_target="tpu_custom_call" | custom-call | tf_op jit(solution)/shard_map/mbconv_forward/pallas_call | solution.py:193
  64.4 0.0 copy-done.13
  64.4 0.0 all-to-all-done
  64.4 7.0 %all-to-all-start.1 = ((bf16[128,8,512]{2,1,0:T(8,128)(2,1)}), bf16[128,8,512]{2,1,0:T(8,128)(2,1)S(1)}, u32[]{:S(2)}, u32[]{:S(2)}) async-start(bf16[128,8,512]{2,1,0:T(8,128)(2,1)} %bitcast.39), calls=%async_computation.1 | async-start | bytes 2097152 | tf_op jit(solution)/shard_map/all_to_all | solution.py:584
  71.5 0.0 copy-start.7
  71.5 15.3 %mbconv_slopes.2 = (f32[1024,2048]{1,0:T(8,128)}, f32[1152,2048]{1,0:T(8,128)}, f32[48,2048]{1,0:T(8,128)}) custom-call(bf16[3,64,512]{2,1,0:T(8,128)(2,1)} %copy.41.top, bf16[16,64,512]{2,1,0:T(8,128)(2,1)} %mid.5, bf16[3,64,512]{2,1,0:T(8,128)(2,1)} %copy.42.bot, bf16[72,512]{1,0:T(8,128)(2,1)} %copy-done.11, bf16[48,512]{1,0:T(8,128)(2,1)} %bitcast.45, ...), custom_call_target="tpu_custom_call" | custom-call | tf_op jit(solution)/shard_map/mbconv_slopes/pallas_call | solution.py:264
  86.8 1.8 %all-to-all-done.1 = bf16[128,8,512]{2,1,0:T(8,128)(2,1)S(1)} async-done(((bf16[128,8,512]{2,1,0:T(8,128)(2,1)}), bf16[128,8,512]{2,1,0:T(8,128)(2,1)S(1)}, u32[]{:S(2)}, u32[]{:S(2)}) %all-to-all-start.1) | async-done | bytes 1048608 | tf_op jit(solution)/shard_map/all_to_all | solution.py:584
  88.6 1.4 copy-done.1
  90.0 19.5 %window_attention.1 = (bf16[5120,128]{1,0:T(8,128)(2,1)}, bf16[1024,512]{1,0:T(8,128)(2,1)S(1)}) custom-call(s32[2]{0:T(128)S(1)} %copy-done.5, bf16[1024,512]{1,0:T(8,128)(2,1)S(1)} %bitcast.33, bf16[1024,512]{1,0:T(8,128)(2,1)S(1)} %bitcast.32, f32[1,512]{1,0:T(1,128)S(1)} %bitcast.35, bf16[512,1536]{1,0:T(8,128)(2,1)S(1)} %copy-done.1), custom_call_target="tpu_custom_call" | custom-call | tf_op jit(solution)/shard_map/window_attention/pallas_call | solution.py:531
  109.4 1.0 copy-done.8
  110.4 8.0 %all-to-all-start.2 = ((bf16[128,40,128]{2,1,0:T(8,128)(2,1)}), bf16[128,40,128]{2,1,0:T(8,128)(2,1)S(1)}, u32[]{:S(2)}, u32[]{:S(2)}) async-start(bf16[128,40,128]{2,1,0:T(8,128)(2,1)} %bitcast.16), calls=%async_computation.2 | async-start | bytes 2621440 | tf_op jit(solution)/shard_map/all_to_all | solution.py:584
  118.4 0.0 copy-start.9
  118.4 10.4 %mbconv_slopes.3 = (f32[1024,2048]{1,0:T(8,128)}, f32[1152,2048]{1,0:T(8,128)}, f32[48,2048]{1,0:T(8,128)}) custom-call(bf16[3,64,512]{2,1,0:T(8,128)(2,1)} %copy.41.top, bf16[16,64,512]{2,1,0:T(8,128)(2,1)} %mid.5, bf16[3,64,512]{2,1,0:T(8,128)(2,1)} %copy.42.bot, ...), custom_call_target="tpu_custom_call", output_to_operand_aliasing={{0}: (9, {}), {1}: (10, {}), {2}: (11, {})} | custom-call | tf_op jit(solution)/shard_map/mbconv_slopes/pallas_call | solution.py:264
  128.8 1.7 %convolution_convert_fusion = bf16[1024,512]{1,0:T(8,128)(2,1)} fusion(bf16[1024,512]{1,0:T(8,128)(2,1)S(1)} %copy-done.9, bf16[512,512]{1,0:T(8,128)(2,1)S(1)} %copy-done.3), kind=kOutput, calls=%fused_computation | convolution fusion | flops 537395200 | bytes 2621440 | tf_op jit(solution)/shard_map/dot_general | solution.py:623
  130.5 7.8 %all-to-all-done.2 = bf16[128,40,128]{2,1,0:T(8,128)(2,1)S(1)} async-done(((bf16[128,40,128]{2,1,0:T(8,128)(2,1)}), bf16[128,40,128]{2,1,0:T(8,128)(2,1)S(1)}, u32[]{:S(2)}, u32[]{:S(2)}) %all-to-all-start.2) | async-done | bytes 1310752 | tf_op jit(solution)/shard_map/all_to_all | solution.py:584
  138.3 1.1 copy-done.10
  139.4 6.5 %all-to-all-start.3 = ((bf16[128,8,512]{2,1,0:T(8,128)(2,1)}), bf16[128,8,512]{2,1,0:T(8,128)(2,1)S(1)}, u32[]{:S(2)}, u32[]{:S(2)}) async-start(bf16[128,8,512]{2,1,0:T(8,128)(2,1)} %bitcast.38), calls=%async_computation.3 | async-start | bytes 2097152 | tf_op jit(solution)/shard_map/all_to_all | solution.py:584
  145.9 0.0 copy-start.2
  145.9 19.7 %mbconv_backward.1 = bf16[1024,512]{1,0:T(8,128)(2,1)} custom-call(s32[2]{0:T(128)} %copy-done.4, bf16[3,64,512]{2,1,0:T(8,128)(2,1)} %copy.41.top, bf16[1024,512]{1,0:T(8,128)(2,1)} %bitcast.30, bf16[5120,128]{1,0:T(8,128)(2,1)} %bitcast.36, bf16[3,64,512]{2,1,0:T(8,128)(2,1)} %copy.42.bot, bf16[72,512]{1,0:T(8,128)(2,1)} %copy-done.11, ...), custom_call_target="tpu_custom_call" | custom-call | tf_op jit(solution)/shard_map/mbconv_backward/pallas_call | solution.py:357
  165.7 0.0 all-to-all-done.3
  165.7 2.3 %add_attention.1 = bf16[1024,512]{1,0:T(8,128)(2,1)} custom-call(s32[2]{0:T(128)S(1)} %copy-done.6, bf16[1024,512]{1,0:T(8,128)(2,1)S(1)} %copy-done.2, bf16[1024,512]{1,0:T(8,128)(2,1)S(1)} %bitcast.34), custom_call_target="tpu_custom_call" | custom-call | tf_op jit(solution)/shard_map/add_attention/pallas_call | solution.py:137
  (35 shorter events, 0.2 us)
Async XLA Ops:
  0.6 9.1 %copy-start = (bf16[16,64,512]{2,1,0:T(8,128)(2,1)S(1)}, bf16[16,64,512]{2,1,0:T(8,128)(2,1)}, u32[]{:S(2)}) copy-start(bf16[16,64,512]{2,1,0:T(8,128)(2,1)} %param.9) | copy-start | bytes 3145732
  0.6 10.3 %copy-start.3 = (bf16[512,512]{1,0:T(8,128)(2,1)S(1)}, bf16[512,512]{1,0:T(8,128)(2,1)}, u32[]{:S(2)}) copy-start(bf16[512,512]{1,0:T(8,128)(2,1)} %w_out.1) | copy-start | bytes 1572868
  3.2 13.2 %collective-permute-start = (bf16[3,64,512]{2,0,1:T(4,128)(2,1)S(1)}, bf16[3,64,512]{2,0,1:T(4,128)(2,1)S(1)}, u32[]{:S(2)}, u32[]{:S(2)}) collective-permute-start(bf16[3,64,512]{2,0,1:T(4,128)(2,1)S(1)} %pad_maximum_fusion), channel_id=1, source_target_pairs={{0,8},{8,16},{16,24},{24,32},{32,40},{40,48},{48,56},{56,64},{64,7... | collective-permute-start | bytes 589832 | tf_op jit(solution)/shard_map/ppermute | solution.py:554
  7.8 8.6 %collective-permute-start.1 = (bf16[3,64,512]{2,0,1:T(4,128)(2,1)S(1)}, bf16[3,64,512]{2,0,1:T(4,128)(2,1)S(1)}, u32[]{:S(2)}, u32[]{:S(2)}) collective-permute-start(bf16[3,64,512]{2,0,1:T(4,128)(2,1)S(1)} %pad_maximum_fusion.1), channel_id=1, source_target_pairs={{8,0},{16,8},{24,16},{32,24},{40,32},{48,40},{56,48},{64,56},{72,6... | collective-permute-start | bytes 589832 | tf_op jit(solution)/shard_map/ppermute | solution.py:554
  11.0 5.7 %copy-start.4 = (s32[2]{0:T(128)}, s32[2]{0:T(128)S(1)}, u32[]{:S(2)}) copy-start(s32[2]{0:T(128)S(1)} %pad_add_fusion.place) | copy-start | bytes 28
  16.5 47.9 %copy-start.13 = (bf16[2,24,512]{2,1,0:T(8,128)(2,1)}, bf16[2,24,512]{2,1,0:T(8,128)(2,1)S(1)}, u32[]{:S(2)}) copy-start(bf16[2,24,512]{2,1,0:T(8,128)(2,1)S(1)} %pad.14) | copy-start | bytes 147460
  16.6 47.8 %copy-start.14 = (bf16[2,24,512]{2,1,0:T(8,128)(2,1)}, bf16[2,24,512]{2,1,0:T(8,128)(2,1)S(1)}, u32[]{:S(2)}) copy-start(bf16[2,24,512]{2,1,0:T(8,128)(2,1)S(1)} %pad.16) | copy-start | bytes 147460
  16.6 47.8 %all-to-all-start = ((bf16[128,8,512]{2,1,0:T(8,128)(2,1)}), bf16[128,8,512]{2,1,0:T(8,128)(2,1)S(1)}, u32[]{:S(2)}, u32[]{:S(2)}) async-start(bf16[128,8,512]{2,1,0:T(8,128)(2,1)} %bitcast.11), calls=%async_computation | async-start | bytes 2097152 | tf_op jit(solution)/shard_map/all_to_all | solution.py:584
  26.3 17.0 %collective-permute-start.2 = (bf16[72,512]{1,0:T(8,128)(2,1)S(1)}, bf16[72,512]{1,0:T(8,128)(2,1)S(1)}, u32[]{:S(2)}, u32[]{:S(2)}) collective-permute-start(bf16[72,512]{1,0:T(8,128)(2,1)S(1)} %pad_maximum_fusion.2), channel_id=1, source_target_pairs={{0,1},{1,2},{2,3},{3,4},{4,5},{5,6},{6,7},{8,9},{9,10},{10,11},{11... | collective-permute-start | bytes 221192 | tf_op jit(solution)/shard_map/ppermute | solution.py:554
  29.5 13.7 %collective-permute-start.3 = (bf16[72,512]{1,0:T(8,128)(2,1)S(1)}, bf16[72,512]{1,0:T(8,128)(2,1)S(1)}, u32[]{:S(2)}, u32[]{:S(2)}) collective-permute-start(bf16[72,512]{1,0:T(8,128)(2,1)S(1)} %pad_maximum_fusion.3), channel_id=1, source_target_pairs={{1,0},{2,1},{3,2},{4,3},{5,4},{6,5},{7,6},{9,8},{10,9},{11,10},{12... | collective-permute-start | bytes 221192 | tf_op jit(solution)/shard_map/ppermute | solution.py:554
  43.3 0.6 copy-start.11
  43.9 0.6 copy-start.12
  64.4 24.1 %all-to-all-start.1 = ((bf16[128,8,512]{2,1,0:T(8,128)(2,1)}), bf16[128,8,512]{2,1,0:T(8,128)(2,1)S(1)}, u32[]{:S(2)}, u32[]{:S(2)}) async-start(bf16[128,8,512]{2,1,0:T(8,128)(2,1)} %bitcast.39), calls=%async_computation.1 | async-start | bytes 2097152 | tf_op jit(solution)/shard_map/all_to_all | solution.py:584
  71.5 17.1 %copy-start.5 = (s32[2]{0:T(128)S(1)}, s32[2]{0:T(128)}, u32[]{:S(2)}) copy-start(s32[2]{0:T(128)} %copy-done.4) | copy-start | bytes 28
  71.5 17.1 %copy-start.7 = (f32[512]{0:T(512)S(1)}, f32[512]{0:T(512)}, u32[]{:S(2)}) copy-start(f32[512]{0:T(512)} %param.13) | copy-start | bytes 6148
  88.6 1.4 copy-start.1
  109.4 1.0 copy-start.8
  110.4 27.9 %all-to-all-start.2 = ((bf16[128,40,128]{2,1,0:T(8,128)(2,1)}), bf16[128,40,128]{2,1,0:T(8,128)(2,1)S(1)}, u32[]{:S(2)}, u32[]{:S(2)}) async-start(bf16[128,40,128]{2,1,0:T(8,128)(2,1)} %bitcast.16), calls=%async_computation.2 | async-start | bytes 2621440 | tf_op jit(solution)/shard_map/all_to_all | solution.py:584
  118.4 10.4 %copy-start.9 = (bf16[1024,512]{1,0:T(8,128)(2,1)S(1)}, bf16[1024,512]{1,0:T(8,128)(2,1)}, u32[]{:S(2)}) copy-start(bf16[1024,512]{1,0:T(8,128)(2,1)} %copy-done.8) | copy-start | bytes 3145732
  138.3 1.1 copy-start.10
  139.4 26.3 %all-to-all-start.3 = ((bf16[128,8,512]{2,1,0:T(8,128)(2,1)}), bf16[128,8,512]{2,1,0:T(8,128)(2,1)S(1)}, u32[]{:S(2)}, u32[]{:S(2)}) async-start(bf16[128,8,512]{2,1,0:T(8,128)(2,1)} %bitcast.38), calls=%async_computation.3 | async-start | bytes 2097152 | tf_op jit(solution)/shard_map/all_to_all | solution.py:584
  145.9 19.8 %copy-start.2 = (bf16[1024,512]{1,0:T(8,128)(2,1)S(1)}, bf16[1024,512]{1,0:T(8,128)(2,1)}, u32[]{:S(2)}) copy-start(bf16[1024,512]{1,0:T(8,128)(2,1)} %get-tuple-element.33.hidden) | copy-start | bytes 3145732
  145.9 19.8 %copy-start.6 = (s32[2]{0:T(128)S(1)}, s32[2]{0:T(128)}, u32[]{:S(2)}) copy-start(s32[2]{0:T(128)} %copy-done.4) | copy-start | bytes 28

commit v2 on v1

--- a/solution.py
+++ b/solution.py
@@ -77,14 +77,14 @@
     k = 8 * slot
     if k:
         x = jnp.concatenate([x[k:], x[:k]], axis=0)
-    return pltpu.roll(x, (64 - 4 * parity) & 63, 0)
+    return jnp.where(parity == 1, pltpu.roll(x, 60, 0), x)
 
 
 def receive_order(x, slot, parity):
     k = 8 * slot
     if k:
         x = jnp.concatenate([x[64 - k :], x[: 64 - k]], axis=0)
-    return pltpu.roll(x, 4 * parity, 0)
+    return jnp.where(parity == 1, pltpu.roll(x, 4, 0), x)
 
 
 def pack_for_owners(read, parity, packed_rows, out):
@@ -383,7 +383,7 @@
 
 WINDOWS = 16
 GROUP = 4
-BREADTH = 2
+BREADTH = 8
 
 
 def gather_window(src, start):

time: 169 us -> 164 us (0.970)
  Pallas kernels: 90 us -> 84.6 us
    pallas_call x1, Pallas kernels: 19.5 us -> 14.4 us  [attend(): pl.pallas_call(attend_kernel, out_shape=(jax.ShapeDtypeStruct(blocks, jnp...]
  transfers between devices with their start and end apart: 8 -> 8, of which waited for: 4 -> 4; matrix products, arithmetic and copies ran while one was open for 3% -> 3% of each run, Pallas kernels for 41% -> 42%
where the time goes in v2:
time: 164 us; the launch traced here: 163 us
  Pallas kernels  84.6 us (52%)
  starting transfers between devices  46.1 us (28%)
  waiting for transfers between devices  18.9 us (12%)
  local copies, waits for them, and re-layouts  9.84 us (6%)
  matrix products  1.69 us (1%)
    all_to_all x4, starting transfers between devices, exchange(): lax.all_to_all(sent, ('row', 'col'), split_axis=0, concat_axis=0, tiled=T...  31.2 us
    pallas_call x2, Pallas kernels, slopes(): pl.pallas_call(slope_kernel, grid=(count,), out_shape=tuple((jax.ShapeDty...  25.7 us
    pallas_call x1, Pallas kernels, forward(): pl.pallas_call(fwd_kernel, grid=(expand // BLK,), out_shape=(jax.ShapeDty...  19.9 us
    pallas_call x1, Pallas kernels, backward(): pl.pallas_call(bwd_kernel, grid=(expand // BLK,), out_shape=jax.ShapeDtyp...  19.8 us
    ppermute x4, starting transfers between devices, neighbour_pair(): return (lax.ppermute(to_next, axis, up), lax.ppermute(to_prev, axis, down))  14.8 us
    pallas_call x1, Pallas kernels, attend(): pl.pallas_call(attend_kernel, out_shape=(jax.ShapeDtypeStruct(blocks, jnp...  14.4 us
    all_to_all x4, waiting for transfers between devices, exchange(): lax.all_to_all(sent, ('row', 'col'), split_axis=0, concat_axis=0, tiled=T...  9.59 us
    ppermute x4, waiting for transfers between devices, neighbour_pair(): return (lax.ppermute(to_next, axis, up), lax.ppermute(to_prev, axis, down))  9.29 us
  transfers between devices with their start and end apart: 8, of which 4 were waited for; matrix products, arithmetic and copies ran while one was open for 3% of the time, Pallas kernels for 42%

profile of v2, /device:TPU:7, one launch (start us, length us, event | category | flops | bytes accessed | tf_op | source)
XLA Modules:
  0.0 162.8 jit_solution(12081914628187215725)
XLA Ops:
  0.6 0.0 copy-start
  0.7 1.0 fusion.3
  1.7 0.1 copy.50
  1.8 1.0 fusion.2
  2.8 0.1 copy.49
  2.9 0.3 pad_maximum_fusion
  3.2 4.0 %collective-permute-start = (bf16[3,64,512]{2,0,1:T(4,128)(2,1)S(1)}, bf16[3,64,512]{2,0,1:T(4,128)(2,1)S(1)}, u32[]{:S(2)}, u32[]{:S(2)}) collective-permute-start(bf16[3,64,512]{2,0,1:T(4,128)(2,1)S(1)} %pad_maximum_fusion), channel_id=1, source_target_pairs={{0,8},{8,16},{16,24},{24,32},{32,40},{40,48},{48,56},{56,64},{64,7... | collective-permute-start | bytes 589832 | tf_op jit(solution)/shard_map/ppermute | solution.py:554
  7.2 0.1 copy.52
  7.3 0.1 copy.51
  7.5 0.3 pad_maximum_fusion.1
  7.8 1.9 %collective-permute-start.1 = (bf16[3,64,512]{2,0,1:T(4,128)(2,1)S(1)}, bf16[3,64,512]{2,0,1:T(4,128)(2,1)S(1)}, u32[]{:S(2)}, u32[]{:S(2)}) collective-permute-start(bf16[3,64,512]{2,0,1:T(4,128)(2,1)S(1)} %pad_maximum_fusion.1), channel_id=1, source_target_pairs={{8,0},{16,8},{24,16},{32,24},{40,32},{48,40},{56,48},{64,56},{72,6... | collective-permute-start | bytes 589832 | tf_op jit(solution)/shard_map/ppermute | solution.py:554
  9.7 0.1 fusion.1
  9.8 1.0 fusion
  10.9 0.1 pad_add_fusion.place
  11.0 0.0 copy-done.3
  11.0 2.7 %grad_att.1 = bf16[1024,512]{1,0:T(8,128)(2,1)} custom-call(s32[2]{0:T(128)S(1)} %pad_add_fusion.place, bf16[1024,512]{1,0:T(8,128)(2,1)S(1)} %bitcast.31, bf16[512,512]{1,0:T(8,128)(2,1)S(1)} %copy-done.3), custom_call_target="tpu_custom_call" | custom-call | tf_op jit(solution)/shard_map/grad_att/pallas_call | solution.py:110
  13.7 2.7 %collective-permute-done.1 = bf16[3,64,512]{2,0,1:T(4,128)(2,1)S(1)} collective-permute-done((bf16[3,64,512]{2,0,1:T(4,128)(2,1)S(1)}, bf16[3,64,512]{2,0,1:T(4,128)(2,1)S(1)}, u32[]{:S(2)}, u32[]{:S(2)}) %collective-permute-start.1) | collective-permute-done | bytes 196640 | tf_op jit(solution)/shard_map/ppermute | solution.py:554
  16.4 0.0 collective-permute-done
  16.6 9.6 %all-to-all-start = ((bf16[128,8,512]{2,1,0:T(8,128)(2,1)}), bf16[128,8,512]{2,1,0:T(8,128)(2,1)S(1)}, u32[]{:S(2)}, u32[]{:S(2)}) async-start(bf16[128,8,512]{2,1,0:T(8,128)(2,1)} %bitcast.11), calls=%async_computation | async-start | bytes 2097152 | tf_op jit(solution)/shard_map/all_to_all | solution.py:584
  26.3 3.3 %collective-permute-start.2 = (bf16[72,512]{1,0:T(8,128)(2,1)S(1)}, bf16[72,512]{1,0:T(8,128)(2,1)S(1)}, u32[]{:S(2)}, u32[]{:S(2)}) collective-permute-start(bf16[72,512]{1,0:T(8,128)(2,1)S(1)} %pad_maximum_fusion.2), channel_id=1, source_target_pairs={{0,1},{1,2},{2,3},{3,4},{4,5},{5,6},{6,7},{8,9},{9,10},{10,11},{11... | collective-permute-start | bytes 221192 | tf_op jit(solution)/shard_map/ppermute | solution.py:554
  29.5 5.6 %collective-permute-start.3 = (bf16[72,512]{1,0:T(8,128)(2,1)S(1)}, bf16[72,512]{1,0:T(8,128)(2,1)S(1)}, u32[]{:S(2)}, u32[]{:S(2)}) collective-permute-start(bf16[72,512]{1,0:T(8,128)(2,1)S(1)} %pad_maximum_fusion.3), channel_id=1, source_target_pairs={{1,0},{2,1},{3,2},{4,3},{5,4},{6,5},{7,6},{9,8},{10,9},{11,10},{12... | collective-permute-start | bytes 221192 | tf_op jit(solution)/shard_map/ppermute | solution.py:554
  35.2 0.7 copy.41.top
  35.9 0.8 copy.42.bot
  36.6 6.6 %collective-permute-done.2.left = bf16[72,512]{1,0:T(8,128)(2,1)S(1)} collective-permute-done((bf16[72,512]{1,0:T(8,128)(2,1)S(1)}, bf16[72,512]{1,0:T(8,128)(2,1)S(1)}, u32[]{:S(2)}, u32[]{:S(2)}) %collective-permute-start.2) | collective-permute-done | bytes 73760 | tf_op jit(solution)/shard_map/ppermute | solution.py:554
  43.3 0.0 collective-permute-done.3.right
  43.3 0.6 copy-done.11
  43.9 0.6 copy-done.12
  44.5 19.9 %mbconv_forward.1 = (bf16[1024,512]{1,0:T(8,128)(2,1)}, bf16[1024,512]{1,0:T(8,128)(2,1)}) custom-call(s32[2]{0:T(128)} %copy-done.4, bf16[3,64,512]{2,1,0:T(8,128)(2,1)} %copy.41.top, bf16[16,64,512]{2,1,0:T(8,128)(2,1)} %mid.5, bf16[3,64,512]{2,1,0:T(8,128)(2,1)} %copy.42.bot, bf16[72,512]{1,0:T(8,128)(2,1)} %copy-done.11, bf16[72,512]{1,0:T(8,128)(2,1)} %copy-done.12, ...), custom_call_target="tpu_custom_call" | custom-call | tf_op jit(solution)/shard_map/mbconv_forward/pallas_call | solution.py:193
  64.4 0.0 copy-done.14
  64.4 0.0 all-to-all-done
  64.4 7.0 %all-to-all-start.1 = ((bf16[128,8,512]{2,1,0:T(8,128)(2,1)}), bf16[128,8,512]{2,1,0:T(8,128)(2,1)S(1)}, u32[]{:S(2)}, u32[]{:S(2)}) async-start(bf16[128,8,512]{2,1,0:T(8,128)(2,1)} %bitcast.39), calls=%async_computation.1 | async-start | bytes 2097152 | tf_op jit(solution)/shard_map/all_to_all | solution.py:584
  71.5 0.0 copy-start.7
  71.5 15.3 %mbconv_slopes.2 = (f32[1024,2048]{1,0:T(8,128)}, f32[1152,2048]{1,0:T(8,128)}, f32[48,2048]{1,0:T(8,128)}) custom-call(bf16[3,64,512]{2,1,0:T(8,128)(2,1)} %copy.41.top, bf16[16,64,512]{2,1,0:T(8,128)(2,1)} %mid.5, bf16[3,64,512]{2,1,0:T(8,128)(2,1)} %copy.42.bot, bf16[72,512]{1,0:T(8,128)(2,1)} %copy-done.11, bf16[48,512]{1,0:T(8,128)(2,1)} %bitcast.45, ...), custom_call_target="tpu_custom_call" | custom-call | tf_op jit(solution)/shard_map/mbconv_slopes/pallas_call | solution.py:264
  86.7 1.8 %all-to-all-done.1 = bf16[128,8,512]{2,1,0:T(8,128)(2,1)S(1)} async-done(((bf16[128,8,512]{2,1,0:T(8,128)(2,1)}), bf16[128,8,512]{2,1,0:T(8,128)(2,1)S(1)}, u32[]{:S(2)}, u32[]{:S(2)}) %all-to-all-start.1) | async-done | bytes 1048608 | tf_op jit(solution)/shard_map/all_to_all | solution.py:584
  88.5 1.4 copy-done.1
  89.9 14.4 %window_attention.1 = (bf16[5120,128]{1,0:T(8,128)(2,1)}, bf16[1024,512]{1,0:T(8,128)(2,1)S(1)}) custom-call(s32[2]{0:T(128)S(1)} %copy-done.5, bf16[1024,512]{1,0:T(8,128)(2,1)S(1)} %bitcast.33, bf16[1024,512]{1,0:T(8,128)(2,1)S(1)} %bitcast.32, f32[1,512]{1,0:T(1,128)S(1)} %bitcast.35, bf16[512,1536]{1,0:T(8,128)(2,1)S(1)} %copy-done.1), custom_call_target="tpu_custom_call" | custom-call | tf_op jit(solution)/shard_map/window_attention/pallas_call | solution.py:531
  104.4 1.0 copy-done.8
  105.3 8.0 %all-to-all-start.2 = ((bf16[128,40,128]{2,1,0:T(8,128)(2,1)}), bf16[128,40,128]{2,1,0:T(8,128)(2,1)S(1)}, u32[]{:S(2)}, u32[]{:S(2)}) async-start(bf16[128,40,128]{2,1,0:T(8,128)(2,1)} %bitcast.16), calls=%async_computation.2 | async-start | bytes 2621440 | tf_op jit(solution)/shard_map/all_to_all | solution.py:584
  113.3 0.0 copy-start.9
  113.4 10.4 %mbconv_slopes.3 = (f32[1024,2048]{1,0:T(8,128)}, f32[1152,2048]{1,0:T(8,128)}, f32[48,2048]{1,0:T(8,128)}) custom-call(bf16[3,64,512]{2,1,0:T(8,128)(2,1)} %copy.41.top, bf16[16,64,512]{2,1,0:T(8,128)(2,1)} %mid.5, bf16[3,64,512]{2,1,0:T(8,128)(2,1)} %copy.42.bot, ...), custom_call_target="tpu_custom_call", output_to_operand_aliasing={{0}: (9, {}), {1}: (10, {}), {2}: (11, {})} | custom-call | tf_op jit(solution)/shard_map/mbconv_slopes/pallas_call | solution.py:264
  123.8 1.7 %convolution_convert_fusion = bf16[1024,512]{1,0:T(8,128)(2,1)} fusion(bf16[1024,512]{1,0:T(8,128)(2,1)S(1)} %copy-done.9, bf16[512,512]{1,0:T(8,128)(2,1)S(1)} %copy-done.3), kind=kOutput, calls=%fused_computation | convolution fusion | flops 537395200 | bytes 2621440 | tf_op jit(solution)/shard_map/dot_general | solution.py:623
  125.4 7.8 %all-to-all-done.2 = bf16[128,40,128]{2,1,0:T(8,128)(2,1)S(1)} async-done(((bf16[128,40,128]{2,1,0:T(8,128)(2,1)}), bf16[128,40,128]{2,1,0:T(8,128)(2,1)S(1)}, u32[]{:S(2)}, u32[]{:S(2)}) %all-to-all-start.2) | async-done | bytes 1310752 | tf_op jit(solution)/shard_map/all_to_all | solution.py:584
  133.2 1.1 copy-done.10
  134.3 6.5 %all-to-all-start.3 = ((bf16[128,8,512]{2,1,0:T(8,128)(2,1)}), bf16[128,8,512]{2,1,0:T(8,128)(2,1)S(1)}, u32[]{:S(2)}, u32[]{:S(2)}) async-start(bf16[128,8,512]{2,1,0:T(8,128)(2,1)} %bitcast.38), calls=%async_computation.3 | async-start | bytes 2097152 | tf_op jit(solution)/shard_map/all_to_all | solution.py:584
  140.8 0.0 copy-start.2
  140.9 19.8 %mbconv_backward.1 = bf16[1024,512]{1,0:T(8,128)(2,1)} custom-call(s32[2]{0:T(128)} %copy-done.4, bf16[3,64,512]{2,1,0:T(8,128)(2,1)} %copy.41.top, bf16[1024,512]{1,0:T(8,128)(2,1)} %bitcast.30, bf16[5120,128]{1,0:T(8,128)(2,1)} %bitcast.36, bf16[3,64,512]{2,1,0:T(8,128)(2,1)} %copy.42.bot, bf16[72,512]{1,0:T(8,128)(2,1)} %copy-done.11, ...), custom_call_target="tpu_custom_call" | custom-call | tf_op jit(solution)/shard_map/mbconv_backward/pallas_call | solution.py:357
  160.6 0.0 all-to-all-done.3
  160.7 2.2 %add_attention.1 = bf16[1024,512]{1,0:T(8,128)(2,1)} custom-call(s32[2]{0:T(128)S(1)} %copy-done.6, bf16[1024,512]{1,0:T(8,128)(2,1)S(1)} %copy-done.2, bf16[1024,512]{1,0:T(8,128)(2,1)S(1)} %bitcast.34), custom_call_target="tpu_custom_call" | custom-call | tf_op jit(solution)/shard_map/add_attention/pallas_call | solution.py:137
  (35 shorter events, 0.2 us)
Async XLA Ops:
  0.6 9.1 %copy-start = (bf16[16,64,512]{2,1,0:T(8,128)(2,1)S(1)}, bf16[16,64,512]{2,1,0:T(8,128)(2,1)}, u32[]{:S(2)}) copy-start(bf16[16,64,512]{2,1,0:T(8,128)(2,1)} %param.9) | copy-start | bytes 3145732
  0.6 10.3 %copy-start.3 = (bf16[512,512]{1,0:T(8,128)(2,1)S(1)}, bf16[512,512]{1,0:T(8,128)(2,1)}, u32[]{:S(2)}) copy-start(bf16[512,512]{1,0:T(8,128)(2,1)} %w_out.1) | copy-start | bytes 1572868
  3.2 13.2 %collective-permute-start = (bf16[3,64,512]{2,0,1:T(4,128)(2,1)S(1)}, bf16[3,64,512]{2,0,1:T(4,128)(2,1)S(1)}, u32[]{:S(2)}, u32[]{:S(2)}) collective-permute-start(bf16[3,64,512]{2,0,1:T(4,128)(2,1)S(1)} %pad_maximum_fusion), channel_id=1, source_target_pairs={{0,8},{8,16},{16,24},{24,32},{32,40},{40,48},{48,56},{56,64},{64,7... | collective-permute-start | bytes 589832 | tf_op jit(solution)/shard_map/ppermute | solution.py:554
  7.8 8.6 %collective-permute-start.1 = (bf16[3,64,512]{2,0,1:T(4,128)(2,1)S(1)}, bf16[3,64,512]{2,0,1:T(4,128)(2,1)S(1)}, u32[]{:S(2)}, u32[]{:S(2)}) collective-permute-start(bf16[3,64,512]{2,0,1:T(4,128)(2,1)S(1)} %pad_maximum_fusion.1), channel_id=1, source_target_pairs={{8,0},{16,8},{24,16},{32,24},{40,32},{48,40},{56,48},{64,56},{72,6... | collective-permute-start | bytes 589832 | tf_op jit(solution)/shard_map/ppermute | solution.py:554
  11.0 5.7 %copy-start.4 = (s32[2]{0:T(128)}, s32[2]{0:T(128)S(1)}, u32[]{:S(2)}) copy-start(s32[2]{0:T(128)S(1)} %pad_add_fusion.place) | copy-start | bytes 28
  16.5 47.8 %copy-start.13 = (bf16[2,24,512]{2,1,0:T(8,128)(2,1)}, bf16[2,24,512]{2,1,0:T(8,128)(2,1)S(1)}, u32[]{:S(2)}) copy-start(bf16[2,24,512]{2,1,0:T(8,128)(2,1)S(1)} %pad.14) | copy-start | bytes 147460
  16.6 47.8 %copy-start.14 = (bf16[2,24,512]{2,1,0:T(8,128)(2,1)}, bf16[2,24,512]{2,1,0:T(8,128)(2,1)S(1)}, u32[]{:S(2)}) copy-start(bf16[2,24,512]{2,1,0:T(8,128)(2,1)S(1)} %pad.16) | copy-start | bytes 147460
  16.6 47.8 %all-to-all-start = ((bf16[128,8,512]{2,1,0:T(8,128)(2,1)}), bf16[128,8,512]{2,1,0:T(8,128)(2,1)S(1)}, u32[]{:S(2)}, u32[]{:S(2)}) async-start(bf16[128,8,512]{2,1,0:T(8,128)(2,1)} %bitcast.11), calls=%async_computation | async-start | bytes 2097152 | tf_op jit(solution)/shard_map/all_to_all | solution.py:584
  26.3 17.0 %collective-permute-start.2 = (bf16[72,512]{1,0:T(8,128)(2,1)S(1)}, bf16[72,512]{1,0:T(8,128)(2,1)S(1)}, u32[]{:S(2)}, u32[]{:S(2)}) collective-permute-start(bf16[72,512]{1,0:T(8,128)(2,1)S(1)} %pad_maximum_fusion.2), channel_id=1, source_target_pairs={{0,1},{1,2},{2,3},{3,4},{4,5},{5,6},{6,7},{8,9},{9,10},{10,11},{11... | collective-permute-start | bytes 221192 | tf_op jit(solution)/shard_map/ppermute | solution.py:554
  29.5 13.7 %collective-permute-start.3 = (bf16[72,512]{1,0:T(8,128)(2,1)S(1)}, bf16[72,512]{1,0:T(8,128)(2,1)S(1)}, u32[]{:S(2)}, u32[]{:S(2)}) collective-permute-start(bf16[72,512]{1,0:T(8,128)(2,1)S(1)} %pad_maximum_fusion.3), channel_id=1, source_target_pairs={{1,0},{2,1},{3,2},{4,3},{5,4},{6,5},{7,6},{9,8},{10,9},{11,10},{12... | collective-permute-start | bytes 221192 | tf_op jit(solution)/shard_map/ppermute | solution.py:554
  43.3 0.6 copy-start.11
  43.9 0.6 copy-start.12
  64.4 24.1 %all-to-all-start.1 = ((bf16[128,8,512]{2,1,0:T(8,128)(2,1)}), bf16[128,8,512]{2,1,0:T(8,128)(2,1)S(1)}, u32[]{:S(2)}, u32[]{:S(2)}) async-start(bf16[128,8,512]{2,1,0:T(8,128)(2,1)} %bitcast.39), calls=%async_computation.1 | async-start | bytes 2097152 | tf_op jit(solution)/shard_map/all_to_all | solution.py:584
  71.5 17.1 %copy-start.5 = (s32[2]{0:T(128)S(1)}, s32[2]{0:T(128)}, u32[]{:S(2)}) copy-start(s32[2]{0:T(128)} %copy-done.4) | copy-start | bytes 28
  71.5 17.1 %copy-start.7 = (f32[512]{0:T(512)S(1)}, f32[512]{0:T(512)}, u32[]{:S(2)}) copy-start(f32[512]{0:T(512)} %param.13) | copy-start | bytes 6148
  88.5 1.4 copy-start.1
  104.4 1.0 copy-start.8
  105.3 27.9 %all-to-all-start.2 = ((bf16[128,40,128]{2,1,0:T(8,128)(2,1)}), bf16[128,40,128]{2,1,0:T(8,128)(2,1)S(1)}, u32[]{:S(2)}, u32[]{:S(2)}) async-start(bf16[128,40,128]{2,1,0:T(8,128)(2,1)} %bitcast.16), calls=%async_computation.2 | async-start | bytes 2621440 | tf_op jit(solution)/shard_map/all_to_all | solution.py:584
  113.3 10.4 %copy-start.9 = (bf16[1024,512]{1,0:T(8,128)(2,1)S(1)}, bf16[1024,512]{1,0:T(8,128)(2,1)}, u32[]{:S(2)}) copy-start(bf16[1024,512]{1,0:T(8,128)(2,1)} %copy-done.8) | copy-start | bytes 3145732
  133.2 1.1 copy-start.10
  134.3 26.3 %all-to-all-start.3 = ((bf16[128,8,512]{2,1,0:T(8,128)(2,1)}), bf16[128,8,512]{2,1,0:T(8,128)(2,1)S(1)}, u32[]{:S(2)}, u32[]{:S(2)}) async-start(bf16[128,8,512]{2,1,0:T(8,128)(2,1)} %bitcast.38), calls=%async_computation.3 | async-start | bytes 2097152 | tf_op jit(solution)/shard_map/all_to_all | solution.py:584
  140.8 19.8 %copy-start.2 = (bf16[1024,512]{1,0:T(8,128)(2,1)S(1)}, bf16[1024,512]{1,0:T(8,128)(2,1)}, u32[]{:S(2)}) copy-start(bf16[1024,512]{1,0:T(8,128)(2,1)} %get-tuple-element.33.hidden) | copy-start | bytes 3145732
  140.9 19.8 %copy-start.6 = (s32[2]{0:T(128)S(1)}, s32[2]{0:T(128)}, u32[]{:S(2)}) copy-start(s32[2]{0:T(128)} %copy-done.4) | copy-start | bytes 28

commit v3 on v2

--- a/solution.py
+++ b/solution.py
@@ -9,6 +9,7 @@
 C0 = 0.7978845608028654
 C1 = C0 * 0.044715
 BLK = 256
+WIDE = 512
 FRAME = 80
 EDGE = 24
 LIMIT = 60 * 1024 * 1024
@@ -40,12 +41,12 @@
 
 
 def put_rows(dst, values, row, count):
-    for part in range(BLK // 128):
+    for part in range(values.shape[1] // 128):
         dst[part, row : row + count, 8:72, :] = values[:, lanes_of(part)].reshape(count, 64, 128)
 
 
 def put_edge(dst, values, first, count, col):
-    for part in range(BLK // 128):
+    for part in range(values.shape[1] // 128):
         for r in range(count):
             dst[part, r, col : col + 1, :] = values[first + r : first + r + 1, lanes_of(part)]
 
@@ -166,7 +167,7 @@
         put_rows(act, act_of(mid[r : r + 4].reshape(256, width)), 1 + r, 4)
     put_rows(act, act_of(bot[0]), 17, 1)
 
-    for part in range(BLK // 128):
+    for part in range(WIDE // 128):
         taps = read_taps(dw, part, False)
         for r in range(16):
             h = conv_row(act, part, r, taps)
@@ -192,20 +193,20 @@
     width, expand = w_exp.shape
     return pl.pallas_call(
         fwd_kernel,
-        grid=(expand // BLK,),
+        grid=(expand // WIDE,),
         out_shape=(jax.ShapeDtypeStruct((1024, width), jnp.bfloat16),) * 2,
         in_specs=[
             SMEM, full(top.shape), full(mid.shape), full(bot.shape), full(left.shape),
             full(right.shape),
-            pl.BlockSpec((width, BLK), lambda i: (0, i)),
-            pl.BlockSpec((3, 3, BLK), lambda i: (0, 0, i)),
-            pl.BlockSpec((BLK, width), lambda i: (i, 0)),
+            pl.BlockSpec((width, WIDE), lambda i: (0, i)),
+            pl.BlockSpec((3, 3, WIDE), lambda i: (0, 0, i)),
+            pl.BlockSpec((WIDE, width), lambda i: (i, 0)),
         ],
         out_specs=(full((1024, width)),) * 2,
         scratch_shapes=[
-            pltpu.VMEM((BLK // 128, 18, FRAME, 128), jnp.float32),
+            pltpu.VMEM((WIDE // 128, 18, FRAME, 128), jnp.float32),
             pltpu.VMEM((1024, width), jnp.float32),
-            pltpu.VMEM((1024, BLK), jnp.bfloat16),
+            pltpu.VMEM((1024, WIDE), jnp.bfloat16),
             pltpu.VMEM((4, 1024, 128), jnp.float32),
         ],
         name="mbconv_forward",
@@ -337,7 +338,7 @@
         put(rounded[r * 64 : r * 64 + 256], 1 + r, 4)
     put(ends[64:128], 17, 1)
 
-    for part in range(BLK // 128):
+    for part in range(WIDE // 128):
         taps = read_taps(dw, part, True)
         for r in range(16):
             rows = slice(r * 64, r * 64 + 64)
@@ -356,20 +357,20 @@
     width, expand = w_exp.shape
     return pl.pallas_call(
         bwd_kernel,
-        grid=(expand // BLK,),
+        grid=(expand // WIDE,),
         out_shape=jax.ShapeDtypeStruct((1024, width), jnp.bfloat16),
         in_specs=[
             SMEM, full(top.shape), full(grad.shape), full(back.shape), full(bot.shape),
             full(left.shape), full(right.shape),
-            *(pl.BlockSpec((x.shape[0], BLK), lambda i: (0, i)) for x in tables),
-            pl.BlockSpec((width, BLK), lambda i: (0, i)),
-            pl.BlockSpec((3, 3, BLK), lambda i: (0, 0, i)),
-            pl.BlockSpec((BLK, width), lambda i: (i, 0)),
+            *(pl.BlockSpec((x.shape[0], WIDE), lambda i: (0, i)) for x in tables),
+            pl.BlockSpec((width, WIDE), lambda i: (0, i)),
+            pl.BlockSpec((3, 3, WIDE), lambda i: (0, 0, i)),
+            pl.BlockSpec((WIDE, width), lambda i: (i, 0)),
         ],
         out_specs=full((1024, width)),
         scratch_shapes=[
-            pltpu.VMEM((BLK // 128, 18, FRAME, 128), jnp.float32),
-            pltpu.VMEM((1024, BLK), jnp.bfloat16),
+            pltpu.VMEM((WIDE // 128, 18, FRAME, 128), jnp.float32),
+            pltpu.VMEM((1024, WIDE), jnp.bfloat16),
             pltpu.VMEM((1024, width), jnp.float32),
             pltpu.VMEM((1024, width), jnp.bfloat16),
             pltpu.VMEM(back.shape, jnp.float32),

time: 164 us -> 162 us (0.988)
  Pallas kernels: 84.6 us -> 82.7 us
    pallas_call x2, Pallas kernels: 39.6 us -> 37.8 us  [the longest x1 19 us: backward(): pl.pallas_call(bwd_kernel, grid=(expand // WIDE,), out_shape=jax.ShapeDty...]
  transfers between devices with their start and end apart: 8 -> 8, of which waited for: 4 -> 4; matrix products, arithmetic and copies ran while one was open for 3% -> 3% of each run, Pallas kernels for 42% -> 41%
where the time goes in v3:
time: 162 us; the launch traced here: 161 us
  Pallas kernels  82.7 us (51%)
  starting transfers between devices  46.1 us (28%)
  waiting for transfers between devices  18.9 us (12%)
  local copies, waits for them, and re-layouts  9.84 us (6%)
  matrix products  1.69 us (1%)
    all_to_all x4, starting transfers between devices, exchange(): lax.all_to_all(sent, ('row', 'col'), split_axis=0, concat_axis=0, tiled=T...  31.2 us
    pallas_call x2, Pallas kernels, slopes(): pl.pallas_call(slope_kernel, grid=(count,), out_shape=tuple((jax.ShapeDty...  25.7 us
    pallas_call x1, Pallas kernels, backward(): pl.pallas_call(bwd_kernel, grid=(expand // WIDE,), out_shape=jax.ShapeDty...  19 us
    pallas_call x1, Pallas kernels, forward(): pl.pallas_call(fwd_kernel, grid=(expand // WIDE,), out_shape=(jax.ShapeDt...  18.7 us
    ppermute x4, starting transfers between devices, neighbour_pair(): return (lax.ppermute(to_next, axis, up), lax.ppermute(to_prev, axis, down))  14.8 us
    pallas_call x1, Pallas kernels, attend(): pl.pallas_call(attend_kernel, out_shape=(jax.ShapeDtypeStruct(blocks, jnp...  14.4 us
    all_to_all x4, waiting for transfers between devices, exchange(): lax.all_to_all(sent, ('row', 'col'), split_axis=0, concat_axis=0, tiled=T...  9.59 us
    ppermute x4, waiting for transfers between devices, neighbour_pair(): return (lax.ppermute(to_next, axis, up), lax.ppermute(to_prev, axis, down))  9.29 us
  transfers between devices with their start and end apart: 8, of which 4 were waited for; matrix products, arithmetic and copies ran while one was open for 3% of the time, Pallas kernels for 41%

profile of v3, /device:TPU:7, one launch (start us, length us, event | category | flops | bytes accessed | tf_op | source)
XLA Modules:
  0.0 161.0 jit_solution(16548815448822934212)
XLA Ops:
  0.6 0.0 copy-start
  0.7 1.0 fusion.3
  1.7 0.1 copy.50
  1.8 1.0 fusion.2
  2.8 0.1 copy.49
  2.9 0.3 pad_maximum_fusion
  3.2 4.0 %collective-permute-start = (bf16[3,64,512]{2,0,1:T(4,128)(2,1)S(1)}, bf16[3,64,512]{2,0,1:T(4,128)(2,1)S(1)}, u32[]{:S(2)}, u32[]{:S(2)}) collective-permute-start(bf16[3,64,512]{2,0,1:T(4,128)(2,1)S(1)} %pad_maximum_fusion), channel_id=1, source_target_pairs={{0,8},{8,16},{16,24},{24,32},{32,40},{40,48},{48,56},{56,64},{64,7... | collective-permute-start | bytes 589832 | tf_op jit(solution)/shard_map/ppermute | solution.py:555
  7.2 0.1 copy.52
  7.3 0.1 copy.51
  7.5 0.3 pad_maximum_fusion.1
  7.8 1.9 %collective-permute-start.1 = (bf16[3,64,512]{2,0,1:T(4,128)(2,1)S(1)}, bf16[3,64,512]{2,0,1:T(4,128)(2,1)S(1)}, u32[]{:S(2)}, u32[]{:S(2)}) collective-permute-start(bf16[3,64,512]{2,0,1:T(4,128)(2,1)S(1)} %pad_maximum_fusion.1), channel_id=1, source_target_pairs={{8,0},{16,8},{24,16},{32,24},{40,32},{48,40},{56,48},{64,56},{72,6... | collective-permute-start | bytes 589832 | tf_op jit(solution)/shard_map/ppermute | solution.py:555
  9.7 0.1 fusion.1
  9.8 1.0 fusion
  10.9 0.1 pad_add_fusion.place
  11.0 0.0 copy-done.3
  11.0 2.7 %grad_att.1 = bf16[1024,512]{1,0:T(8,128)(2,1)} custom-call(s32[2]{0:T(128)S(1)} %pad_add_fusion.place, bf16[1024,512]{1,0:T(8,128)(2,1)S(1)} %bitcast.31, bf16[512,512]{1,0:T(8,128)(2,1)S(1)} %copy-done.3), custom_call_target="tpu_custom_call" | custom-call | tf_op jit(solution)/shard_map/grad_att/pallas_call | solution.py:111
  13.7 2.7 %collective-permute-done.1 = bf16[3,64,512]{2,0,1:T(4,128)(2,1)S(1)} collective-permute-done((bf16[3,64,512]{2,0,1:T(4,128)(2,1)S(1)}, bf16[3,64,512]{2,0,1:T(4,128)(2,1)S(1)}, u32[]{:S(2)}, u32[]{:S(2)}) %collective-permute-start.1) | collective-permute-done | bytes 196640 | tf_op jit(solution)/shard_map/ppermute | solution.py:555
  16.4 0.0 collective-permute-done
  16.6 9.6 %all-to-all-start = ((bf16[128,8,512]{2,1,0:T(8,128)(2,1)}), bf16[128,8,512]{2,1,0:T(8,128)(2,1)S(1)}, u32[]{:S(2)}, u32[]{:S(2)}) async-start(bf16[128,8,512]{2,1,0:T(8,128)(2,1)} %bitcast.11), calls=%async_computation | async-start | bytes 2097152 | tf_op jit(solution)/shard_map/all_to_all | solution.py:585
  26.3 3.3 %collective-permute-start.2 = (bf16[72,512]{1,0:T(8,128)(2,1)S(1)}, bf16[72,512]{1,0:T(8,128)(2,1)S(1)}, u32[]{:S(2)}, u32[]{:S(2)}) collective-permute-start(bf16[72,512]{1,0:T(8,128)(2,1)S(1)} %pad_maximum_fusion.2), channel_id=1, source_target_pairs={{0,1},{1,2},{2,3},{3,4},{4,5},{5,6},{6,7},{8,9},{9,10},{10,11},{11... | collective-permute-start | bytes 221192 | tf_op jit(solution)/shard_map/ppermute | solution.py:555
  29.5 5.6 %collective-permute-start.3 = (bf16[72,512]{1,0:T(8,128)(2,1)S(1)}, bf16[72,512]{1,0:T(8,128)(2,1)S(1)}, u32[]{:S(2)}, u32[]{:S(2)}) collective-permute-start(bf16[72,512]{1,0:T(8,128)(2,1)S(1)} %pad_maximum_fusion.3), channel_id=1, source_target_pairs={{1,0},{2,1},{3,2},{4,3},{5,4},{6,5},{7,6},{9,8},{10,9},{11,10},{12... | collective-permute-start | bytes 221192 | tf_op jit(solution)/shard_map/ppermute | solution.py:555
  35.2 0.7 copy.41.top
  35.9 0.8 copy.42.bot
  36.6 6.6 %collective-permute-done.2.left = bf16[72,512]{1,0:T(8,128)(2,1)S(1)} collective-permute-done((bf16[72,512]{1,0:T(8,128)(2,1)S(1)}, bf16[72,512]{1,0:T(8,128)(2,1)S(1)}, u32[]{:S(2)}, u32[]{:S(2)}) %collective-permute-start.2) | collective-permute-done | bytes 73760 | tf_op jit(solution)/shard_map/ppermute | solution.py:555
  43.3 0.0 collective-permute-done.3.right
  43.3 0.6 copy-done.11
  43.9 0.6 copy-done.12
  44.5 18.7 %mbconv_forward.1 = (bf16[1024,512]{1,0:T(8,128)(2,1)}, bf16[1024,512]{1,0:T(8,128)(2,1)}) custom-call(s32[2]{0:T(128)} %copy-done.4, bf16[3,64,512]{2,1,0:T(8,128)(2,1)} %copy.41.top, bf16[16,64,512]{2,1,0:T(8,128)(2,1)} %mid.5, bf16[3,64,512]{2,1,0:T(8,128)(2,1)} %copy.42.bot, bf16[72,512]{1,0:T(8,128)(2,1)} %copy-done.11, bf16[72,512]{1,0:T(8,128)(2,1)} %copy-done.12, ...), custom_call_target="tpu_custom_call" | custom-call | tf_op jit(solution)/shard_map/mbconv_forward/pallas_call | solution.py:194
  63.2 0.0 copy-done.14
  63.2 0.0 all-to-all-done
  63.3 7.0 %all-to-all-start.1 = ((bf16[128,8,512]{2,1,0:T(8,128)(2,1)}), bf16[128,8,512]{2,1,0:T(8,128)(2,1)S(1)}, u32[]{:S(2)}, u32[]{:S(2)}) async-start(bf16[128,8,512]{2,1,0:T(8,128)(2,1)} %bitcast.39), calls=%async_computation.1 | async-start | bytes 2097152 | tf_op jit(solution)/shard_map/all_to_all | solution.py:585
  70.3 0.0 copy-start.7
  70.3 15.3 %mbconv_slopes.2 = (f32[1024,2048]{1,0:T(8,128)}, f32[1152,2048]{1,0:T(8,128)}, f32[48,2048]{1,0:T(8,128)}) custom-call(bf16[3,64,512]{2,1,0:T(8,128)(2,1)} %copy.41.top, bf16[16,64,512]{2,1,0:T(8,128)(2,1)} %mid.5, bf16[3,64,512]{2,1,0:T(8,128)(2,1)} %copy.42.bot, bf16[72,512]{1,0:T(8,128)(2,1)} %copy-done.11, bf16[48,512]{1,0:T(8,128)(2,1)} %bitcast.45, ...), custom_call_target="tpu_custom_call" | custom-call | tf_op jit(solution)/shard_map/mbconv_slopes/pallas_call | solution.py:265
  85.6 1.8 %all-to-all-done.1 = bf16[128,8,512]{2,1,0:T(8,128)(2,1)S(1)} async-done(((bf16[128,8,512]{2,1,0:T(8,128)(2,1)}), bf16[128,8,512]{2,1,0:T(8,128)(2,1)S(1)}, u32[]{:S(2)}, u32[]{:S(2)}) %all-to-all-start.1) | async-done | bytes 1048608 | tf_op jit(solution)/shard_map/all_to_all | solution.py:585
  87.4 1.4 copy-done.1
  88.8 14.4 %window_attention.1 = (bf16[5120,128]{1,0:T(8,128)(2,1)}, bf16[1024,512]{1,0:T(8,128)(2,1)S(1)}) custom-call(s32[2]{0:T(128)S(1)} %copy-done.5, bf16[1024,512]{1,0:T(8,128)(2,1)S(1)} %bitcast.33, bf16[1024,512]{1,0:T(8,128)(2,1)S(1)} %bitcast.32, f32[1,512]{1,0:T(1,128)S(1)} %bitcast.35, bf16[512,1536]{1,0:T(8,128)(2,1)S(1)} %copy-done.1), custom_call_target="tpu_custom_call" | custom-call | tf_op jit(solution)/shard_map/window_attention/pallas_call | solution.py:532
  103.2 1.0 copy-done.8
  104.2 8.0 %all-to-all-start.2 = ((bf16[128,40,128]{2,1,0:T(8,128)(2,1)}), bf16[128,40,128]{2,1,0:T(8,128)(2,1)S(1)}, u32[]{:S(2)}, u32[]{:S(2)}) async-start(bf16[128,40,128]{2,1,0:T(8,128)(2,1)} %bitcast.16), calls=%async_computation.2 | async-start | bytes 2621440 | tf_op jit(solution)/shard_map/all_to_all | solution.py:585
  112.2 0.0 copy-start.9
  112.2 10.4 %mbconv_slopes.3 = (f32[1024,2048]{1,0:T(8,128)}, f32[1152,2048]{1,0:T(8,128)}, f32[48,2048]{1,0:T(8,128)}) custom-call(bf16[3,64,512]{2,1,0:T(8,128)(2,1)} %copy.41.top, bf16[16,64,512]{2,1,0:T(8,128)(2,1)} %mid.5, bf16[3,64,512]{2,1,0:T(8,128)(2,1)} %copy.42.bot, ...), custom_call_target="tpu_custom_call", output_to_operand_aliasing={{0}: (9, {}), {1}: (10, {}), {2}: (11, {})} | custom-call | tf_op jit(solution)/shard_map/mbconv_slopes/pallas_call | solution.py:265
  122.6 1.7 %convolution_convert_fusion = bf16[1024,512]{1,0:T(8,128)(2,1)} fusion(bf16[1024,512]{1,0:T(8,128)(2,1)S(1)} %copy-done.9, bf16[512,512]{1,0:T(8,128)(2,1)S(1)} %copy-done.3), kind=kOutput, calls=%fused_computation | convolution fusion | flops 537395200 | bytes 2621440 | tf_op jit(solution)/shard_map/dot_general | solution.py:624
  124.3 7.8 %all-to-all-done.2 = bf16[128,40,128]{2,1,0:T(8,128)(2,1)S(1)} async-done(((bf16[128,40,128]{2,1,0:T(8,128)(2,1)}), bf16[128,40,128]{2,1,0:T(8,128)(2,1)S(1)}, u32[]{:S(2)}, u32[]{:S(2)}) %all-to-all-start.2) | async-done | bytes 1310752 | tf_op jit(solution)/shard_map/all_to_all | solution.py:585
  132.1 1.1 copy-done.10
  133.2 6.5 %all-to-all-start.3 = ((bf16[128,8,512]{2,1,0:T(8,128)(2,1)}), bf16[128,8,512]{2,1,0:T(8,128)(2,1)S(1)}, u32[]{:S(2)}, u32[]{:S(2)}) async-start(bf16[128,8,512]{2,1,0:T(8,128)(2,1)} %bitcast.38), calls=%async_computation.3 | async-start | bytes 2097152 | tf_op jit(solution)/shard_map/all_to_all | solution.py:585
  139.7 0.0 copy-start.2
  139.7 19.0 %mbconv_backward.1 = bf16[1024,512]{1,0:T(8,128)(2,1)} custom-call(s32[2]{0:T(128)} %copy-done.4, bf16[3,64,512]{2,1,0:T(8,128)(2,1)} %copy.41.top, bf16[1024,512]{1,0:T(8,128)(2,1)} %bitcast.30, bf16[5120,128]{1,0:T(8,128)(2,1)} %bitcast.36, bf16[3,64,512]{2,1,0:T(8,128)(2,1)} %copy.42.bot, bf16[72,512]{1,0:T(8,128)(2,1)} %copy-done.11, ...), custom_call_target="tpu_custom_call" | custom-call | tf_op jit(solution)/shard_map/mbconv_backward/pallas_call | solution.py:358
  158.8 0.0 all-to-all-done.3
  158.8 2.2 %add_attention.1 = bf16[1024,512]{1,0:T(8,128)(2,1)} custom-call(s32[2]{0:T(128)S(1)} %copy-done.6, bf16[1024,512]{1,0:T(8,128)(2,1)S(1)} %copy-done.2, bf16[1024,512]{1,0:T(8,128)(2,1)S(1)} %bitcast.34), custom_call_target="tpu_custom_call" | custom-call | tf_op jit(solution)/shard_map/add_attention/pallas_call | solution.py:138
  (35 shorter events, 0.2 us)
Async XLA Ops:
  0.6 9.1 %copy-start = (bf16[16,64,512]{2,1,0:T(8,128)(2,1)S(1)}, bf16[16,64,512]{2,1,0:T(8,128)(2,1)}, u32[]{:S(2)}) copy-start(bf16[16,64,512]{2,1,0:T(8,128)(2,1)} %param.9) | copy-start | bytes 3145732
  0.6 10.3 %copy-start.3 = (bf16[512,512]{1,0:T(8,128)(2,1)S(1)}, bf16[512,512]{1,0:T(8,128)(2,1)}, u32[]{:S(2)}) copy-start(bf16[512,512]{1,0:T(8,128)(2,1)} %w_out.1) | copy-start | bytes 1572868
  3.2 13.2 %collective-permute-start = (bf16[3,64,512]{2,0,1:T(4,128)(2,1)S(1)}, bf16[3,64,512]{2,0,1:T(4,128)(2,1)S(1)}, u32[]{:S(2)}, u32[]{:S(2)}) collective-permute-start(bf16[3,64,512]{2,0,1:T(4,128)(2,1)S(1)} %pad_maximum_fusion), channel_id=1, source_target_pairs={{0,8},{8,16},{16,24},{24,32},{32,40},{40,48},{48,56},{56,64},{64,7... | collective-permute-start | bytes 589832 | tf_op jit(solution)/shard_map/ppermute | solution.py:555
  7.8 8.6 %collective-permute-start.1 = (bf16[3,64,512]{2,0,1:T(4,128)(2,1)S(1)}, bf16[3,64,512]{2,0,1:T(4,128)(2,1)S(1)}, u32[]{:S(2)}, u32[]{:S(2)}) collective-permute-start(bf16[3,64,512]{2,0,1:T(4,128)(2,1)S(1)} %pad_maximum_fusion.1), channel_id=1, source_target_pairs={{8,0},{16,8},{24,16},{32,24},{40,32},{48,40},{56,48},{64,56},{72,6... | collective-permute-start | bytes 589832 | tf_op jit(solution)/shard_map/ppermute | solution.py:555
  11.0 5.7 %copy-start.4 = (s32[2]{0:T(128)}, s32[2]{0:T(128)S(1)}, u32[]{:S(2)}) copy-start(s32[2]{0:T(128)S(1)} %pad_add_fusion.place) | copy-start | bytes 28
  16.5 46.7 %copy-start.13 = (bf16[2,24,512]{2,1,0:T(8,128)(2,1)}, bf16[2,24,512]{2,1,0:T(8,128)(2,1)S(1)}, u32[]{:S(2)}) copy-start(bf16[2,24,512]{2,1,0:T(8,128)(2,1)S(1)} %pad.14) | copy-start | bytes 147460
  16.6 46.7 %copy-start.14 = (bf16[2,24,512]{2,1,0:T(8,128)(2,1)}, bf16[2,24,512]{2,1,0:T(8,128)(2,1)S(1)}, u32[]{:S(2)}) copy-start(bf16[2,24,512]{2,1,0:T(8,128)(2,1)S(1)} %pad.16) | copy-start | bytes 147460
  16.6 46.6 %all-to-all-start = ((bf16[128,8,512]{2,1,0:T(8,128)(2,1)}), bf16[128,8,512]{2,1,0:T(8,128)(2,1)S(1)}, u32[]{:S(2)}, u32[]{:S(2)}) async-start(bf16[128,8,512]{2,1,0:T(8,128)(2,1)} %bitcast.11), calls=%async_computation | async-start | bytes 2097152 | tf_op jit(solution)/shard_map/all_to_all | solution.py:585
  26.3 17.0 %collective-permute-start.2 = (bf16[72,512]{1,0:T(8,128)(2,1)S(1)}, bf16[72,512]{1,0:T(8,128)(2,1)S(1)}, u32[]{:S(2)}, u32[]{:S(2)}) collective-permute-start(bf16[72,512]{1,0:T(8,128)(2,1)S(1)} %pad_maximum_fusion.2), channel_id=1, source_target_pairs={{0,1},{1,2},{2,3},{3,4},{4,5},{5,6},{6,7},{8,9},{9,10},{10,11},{11... | collective-permute-start | bytes 221192 | tf_op jit(solution)/shard_map/ppermute | solution.py:555
  29.5 13.7 %collective-permute-start.3 = (bf16[72,512]{1,0:T(8,128)(2,1)S(1)}, bf16[72,512]{1,0:T(8,128)(2,1)S(1)}, u32[]{:S(2)}, u32[]{:S(2)}) collective-permute-start(bf16[72,512]{1,0:T(8,128)(2,1)S(1)} %pad_maximum_fusion.3), channel_id=1, source_target_pairs={{1,0},{2,1},{3,2},{4,3},{5,4},{6,5},{7,6},{9,8},{10,9},{11,10},{12... | collective-permute-start | bytes 221192 | tf_op jit(solution)/shard_map/ppermute | solution.py:555
  43.3 0.6 copy-start.11
  43.9 0.6 copy-start.12
  63.3 24.1 %all-to-all-start.1 = ((bf16[128,8,512]{2,1,0:T(8,128)(2,1)}), bf16[128,8,512]{2,1,0:T(8,128)(2,1)S(1)}, u32[]{:S(2)}, u32[]{:S(2)}) async-start(bf16[128,8,512]{2,1,0:T(8,128)(2,1)} %bitcast.39), calls=%async_computation.1 | async-start | bytes 2097152 | tf_op jit(solution)/shard_map/all_to_all | solution.py:585
  70.3 17.1 %copy-start.5 = (s32[2]{0:T(128)S(1)}, s32[2]{0:T(128)}, u32[]{:S(2)}) copy-start(s32[2]{0:T(128)} %copy-done.4) | copy-start | bytes 28
  70.3 17.1 %copy-start.7 = (f32[512]{0:T(512)S(1)}, f32[512]{0:T(512)}, u32[]{:S(2)}) copy-start(f32[512]{0:T(512)} %param.13) | copy-start | bytes 6148
  87.4 1.4 copy-start.1
  103.2 1.0 copy-start.8
  104.2 27.9 %all-to-all-start.2 = ((bf16[128,40,128]{2,1,0:T(8,128)(2,1)}), bf16[128,40,128]{2,1,0:T(8,128)(2,1)S(1)}, u32[]{:S(2)}, u32[]{:S(2)}) async-start(bf16[128,40,128]{2,1,0:T(8,128)(2,1)} %bitcast.16), calls=%async_computation.2 | async-start | bytes 2621440 | tf_op jit(solution)/shard_map/all_to_all | solution.py:585
  112.2 10.4 %copy-start.9 = (bf16[1024,512]{1,0:T(8,128)(2,1)S(1)}, bf16[1024,512]{1,0:T(8,128)(2,1)}, u32[]{:S(2)}) copy-start(bf16[1024,512]{1,0:T(8,128)(2,1)} %copy-done.8) | copy-start | bytes 3145732
  132.1 1.1 copy-start.10
  133.2 25.6 %all-to-all-start.3 = ((bf16[128,8,512]{2,1,0:T(8,128)(2,1)}), bf16[128,8,512]{2,1,0:T(8,128)(2,1)S(1)}, u32[]{:S(2)}, u32[]{:S(2)}) async-start(bf16[128,8,512]{2,1,0:T(8,128)(2,1)} %bitcast.38), calls=%async_computation.3 | async-start | bytes 2097152 | tf_op jit(solution)/shard_map/all_to_all | solution.py:585
  139.7 19.1 %copy-start.2 = (bf16[1024,512]{1,0:T(8,128)(2,1)S(1)}, bf16[1024,512]{1,0:T(8,128)(2,1)}, u32[]{:S(2)}) copy-start(bf16[1024,512]{1,0:T(8,128)(2,1)} %get-tuple-element.33.hidden) | copy-start | bytes 3145732
  139.7 19.1 %copy-start.6 = (s32[2]{0:T(128)S(1)}, s32[2]{0:T(128)}, u32[]{:S(2)}) copy-start(s32[2]{0:T(128)} %copy-done.4) | copy-start | bytes 28
